TPU v7x, 768 devices: a whole 4x8x12 slice. The times are simulated.
768 devices in a mesh: space: 12 (over z_lo, core), frame: 64 (over z_hi, y, x).
Axes of the slice: x: 4, y: 8, z: 12 (z_hi: 2, z_lo: 6; z = z_hi * 6 + z_lo), core: 2. Of those that a mesh axis runs over, the one named last changes fastest.
Arguments:
- latent: bfloat16 [64, 6144, 1024], P('frame', 'space'), may hold values from -6 to 6
- cond: float32 [3, 1024], replicated, may hold values from -3 to 3
- w_qkv: bfloat16 [1024, 3072], replicated
- w_out: bfloat16 [1024, 1024], replicated, may hold values from -0.1875 to 0.1875
- slot: int32 [6144], P('space'), may hold values from 0 to 511, as said below
- neighbours: int32 [48, 4], P('space'), may hold values from 0 to 47, as said below
- counts: int32 [48], P('space'), may hold values from 1 to 4
Outputs:
- updated: bfloat16 [64, 6144, 1024], P('frame', 'space')
Inputs may be any that keep to these rules, and one draw needn't show every extreme that they name: `slot`: each aligned group of 512 entries is a permutation of its range. `neighbours`: row b lists distinct blocks (b + o) mod 48 with -4 <= o <= 4, the first being b itself.
All inputs are finite; a program needn't handle non-finite values.
Results may differ from a plain program's by a relative error of at most 0.0052.
Values may be sent and summed in bfloat16 or wider, within the bound.
No kernel may reach another device: no remote copies, remote signals or barrier semaphores. Data moves between devices by JAX's collectives and lax.ppermute only.
A program may use at most 64 MiB of HBM per device.

v0:
```python
import jax
import jax.numpy as jnp
from jax import lax
from jax.sharding import PartitionSpec as P

HEADS = 8
MAXNB = 4


def with_halo(cells, sides, width):
    for axis, dim in sides:
        count = lax.axis_size(axis)
        head = lax.slice_in_dim(cells, 0, width, axis=dim)
        tail = lax.slice_in_dim(cells, cells.shape[dim] - width, cells.shape[dim], axis=dim)
        cells = jnp.concatenate(
            [
                lax.ppermute(tail, axis, [(i, (i + 1) % count) for i in range(count)]),
                cells,
                lax.ppermute(head, axis, [((i + 1) % count, i) for i in range(count)]),
            ],
            axis=dim,
        )
    return cells


def grouped_exchange(array, axis, split_dim, concat_dim, work, item_dim, out_dim):
    items = jax.tree.leaves(array)[0].shape[item_dim]
    count = 2 if items % 2 == 0 else 1
    outs = []
    for k in range(count):
        group = jax.tree.map(
            lambda a: lax.slice_in_dim(
                a, k * (items // count), (k + 1) * (items // count), axis=item_dim
            ),
            array,
        )
        outs.append(
            work(
                lax.all_to_all(
                    group, axis, split_axis=split_dim, concat_axis=concat_dim, tiled=True
                )
            )
        )
    return jax.tree.map(lambda *parts: jnp.concatenate(parts, axis=out_dim), *outs)


def softmax_last(scores):
    top = jnp.max(scores, axis=-1, keepdims=True)
    expo = jnp.exp(scores - top)
    return expo / jnp.sum(expo, axis=-1, keepdims=True)


def body(latent, cond, w_qkv, w_out, slot, neighbours, counts):
    tokens = latent.shape[1]
    width = latent.shape[2]
    blocks = neighbours.shape[0]
    block_len = tokens // blocks
    half = width // 2
    head_dim = width // HEADS
    sheads = HEADS // 2
    scale = 1.0 / jnp.sqrt(jnp.float32(head_dim))
    frame_total = lax.axis_size("frame")
    clip_len = min(8, frame_total)
    rows = latent[0].astype(jnp.float32)
    centred = rows - jnp.mean(rows, axis=-1, keepdims=True)
    normed = centred * lax.rsqrt(jnp.mean(centred * centred, axis=-1, keepdims=True) + 1e-06)
    modulated = (normed * (1.0 + cond[1]) + cond[0]).astype(jnp.bfloat16)
    projected = jnp.dot(modulated, w_qkv, preferred_element_type=jnp.float32).astype(jnp.bfloat16)
    query_sp = jnp.take(projected[:, :half], slot, axis=0)
    keyval = jnp.take(
        jnp.concatenate(
            [projected[:, width : width + half], projected[:, 2 * width : 2 * width + half]], axis=1
        ),
        slot,
        axis=0,
    )
    window = with_halo(keyval, (("space", 0),), tokens)
    total_blocks = blocks * lax.axis_size("space")
    first_block = (lax.axis_index("space") - 1) * blocks
    local_ids = jnp.mod(neighbours - first_block, total_blocks)
    valid = jnp.arange(MAXNB, dtype=jnp.int32)[None, :] < counts[:, None]
    query_blocks = query_sp.reshape(blocks, block_len, sheads, head_dim)
    keys = window[:, :half].reshape(3 * tokens, sheads, head_dim)
    vals = window[:, half:].reshape(3 * tokens, sheads, head_dim)
    scores = (
        jnp.einsum("jqhd,khd->jhqk", query_blocks, keys, preferred_element_type=jnp.float32) * scale
    )
    allowed = jnp.any(
        (local_ids[:, :, None] == jnp.arange(3 * blocks, dtype=jnp.int32)[None, None, :])
        & valid[:, :, None],
        axis=1,
    )
    keep = jnp.repeat(allowed, block_len, axis=1)[:, None, None, :]
    weights = softmax_last(jnp.where(keep, scores, -jnp.inf)).astype(jnp.bfloat16)
    attended = jnp.einsum("jhqk,khd->jqhd", weights, vals, preferred_element_type=jnp.float32)
    block_out = attended.astype(jnp.bfloat16).reshape(tokens, half)
    spatial = jnp.zeros_like(block_out).at[slot].set(block_out)
    t_query = projected[:, half:width]
    t_key = projected[:, width + half : 2 * width]
    t_val = projected[:, 2 * width + half :]
    per_dest = tokens // frame_total
    stacked = jnp.concatenate([t_query, t_key, t_val], axis=1).reshape(
        1, frame_total, per_dest, 3 * half
    )

    def attend_frames(group):
        frame_count = group.shape[0]
        count = group.shape[2]
        parts = group.reshape(frame_count, count, 3, sheads, head_dim)
        t_scores = (
            jnp.einsum(
                "fnhd,gnhd->nhfg",
                parts[:, :, 0],
                parts[:, :, 1],
                preferred_element_type=jnp.float32,
            )
            * scale
        )
        clip_of = jnp.arange(frame_count, dtype=jnp.int32) // clip_len
        same_clip = clip_of[:, None] == clip_of[None, :]
        t_weights = softmax_last(jnp.where(same_clip[None, None], t_scores, -jnp.inf))
        result = jnp.einsum(
            "nhfg,gnhd->fnhd",
            t_weights,
            parts[:, :, 2].astype(jnp.float32),
            precision=lax.Precision.HIGHEST,
            preferred_element_type=jnp.float32,
        )
        return result.astype(jnp.bfloat16).reshape(frame_count, 1, count, half)

    mixed_frames = grouped_exchange(stacked, "frame", 1, 0, attend_frames, 2, 2)
    temporal = lax.all_to_all(
        mixed_frames, "frame", split_axis=0, concat_axis=1, tiled=True
    ).reshape(tokens, half)
    joined = jnp.concatenate([spatial, temporal], axis=1)
    mixed = jnp.dot(joined, w_out, preferred_element_type=jnp.float32)
    return (rows + cond[2] * mixed).astype(jnp.bfloat16)[None]


def solution(mesh):
    in_specs = (P("frame", "space", None), P(), P(), P(), P("space"), P("space", None), P("space"))
    out_specs = P("frame", "space", None)
    return jax.shard_map(body, mesh=mesh, in_specs=in_specs, out_specs=out_specs, check_vma=False)
```

profile of v0, /device:TPU:136, one launch (start us, length us, event | category | flops | bytes accessed | tf_op | source)
XLA Modules:
  0.0 177.4 jit_solution(17852148200520933539)
XLA Ops:
  0.0 1.6 convert_reduce_fusion
  1.6 1.6 fusion.10
  3.3 6.7 %convolution_convert_fusion = bf16[512,3072]{1,0:T(8,128)(2,1)S(1)} fusion(bf16[1024,3072]{1,0:T(8,128)(2,1)} %param.9, bf16[1,512,1024]{2,1,0:T(8,128)(2,1)S(1)} %copy-done.2, f32[1024]{0:T(1024)S(1)} %bitcast.118, f32[1024]{0:T(1024)S(1)} %bitcast.119, f32[512]{0:T(512)S(1)} %add_rsqrt_fusion, f32[512]{0:T(512)S(1)} %broadcast_multiply_fusion), kind=kOutput, calls=%fused_computation.12 | convolution fusion | flops 3225944064 | bytes 10498048 | tf_op jit(solution)/shard_map/dot_general | solution.py:68
  10.0 1.2 fusion.58
  11.3 1.7 fusion.60
  13.0 21.0 %all-to-all-start = ((bf16[1,64,4,1536]{3,2,0,1:T(4,128)(2,1)}), bf16[1,64,4,1536]{3,2,0,1:T(4,128)(2,1)}, u32[]{:S(2)}, u32[]{:S(2)}) async-start(bf16[1,64,4,1536]{3,2,0,1:T(4,128)(2,1)} %get-tuple-element.13), calls=%async_computation | async-start | bytes 1572864 | tf_op jit(solution)/shard_map/all_to_all | solution.py:39
  34.0 1.3 pad_maximum_fusion.1
  35.3 2.8 %gather_fusion = bf16[512,1024]{1,0:T(8,128)(2,1)} fusion(bf16[512,1024]{1,0:T(8,128)(2,1)S(1)} %pad_maximum_fusion.1, s32[1024]{0:T(1024)S(1)} %pad_clamp_fusion), kind=kCustom, calls=%fused_computation | custom fusion | bytes 2099200 | tf_op jit(solution)/shard_map/jit(_take)/gather | solution.py:70
  38.1 2.4 %broadcast_select_fusion = bf16[512,1024]{1,0:T(8,128)(2,1)} fusion(bf16[512,1024]{1,0:T(8,128)(2,1)} %gather_fusion, pred[512]{0:T(512)(128)(4,1)S(1)} %compare_and_fusion), kind=kLoop, calls=%fused_computation.46 | loop fusion | flops 524288 | bytes 2097664 | tf_op jit(solution)/shard_map/jit(_take)/select_n | solution.py:70
  40.6 1.9 %collective-permute-start.1 = (bf16[512,1024]{1,0:T(8,128)(2,1)}, bf16[512,1024]{1,0:T(8,128)(2,1)}, u32[]{:S(2)}, u32[]{:S(2)}) collective-permute-start(bf16[512,1024]{1,0:T(8,128)(2,1)} %broadcast_select_fusion), channel_id=1, source_target_pairs={{64,0},{128,64},{192,128},{256,192},{320,256},{384,320},{448,384},... | collective-permute-start | bytes 3145736 | tf_op jit(solution)/shard_map/ppermute | solution.py:19
  42.5 2.4 %collective-permute-start = (bf16[512,1024]{1,0:T(8,128)(2,1)}, bf16[512,1024]{1,0:T(8,128)(2,1)}, u32[]{:S(2)}, u32[]{:S(2)}) collective-permute-start(bf16[512,1024]{1,0:T(8,128)(2,1)} %broadcast_select_fusion), channel_id=1, source_target_pairs={{0,64},{64,128},{128,192},{192,256},{256,320},{320,384},{384,448},... | collective-permute-start | bytes 3145736 | tf_op jit(solution)/shard_map/ppermute | solution.py:17
  45.2 27.6 %all-to-all-done = bf16[1,64,4,1536]{3,2,0,1:T(4,128)(2,1)} async-done(((bf16[1,64,4,1536]{3,2,0,1:T(4,128)(2,1)}), bf16[1,64,4,1536]{3,2,0,1:T(4,128)(2,1)}, u32[]{:S(2)}, u32[]{:S(2)}) %all-to-all-start) | async-done | bytes 786464 | tf_op jit(solution)/shard_map/all_to_all | solution.py:39
  72.8 6.0 %all-to-all-start.1 = ((bf16[1,64,4,1536]{3,2,0,1:T(4,128)(2,1)}), bf16[1,64,4,1536]{3,2,0,1:T(4,128)(2,1)S(1)}, u32[]{:S(2)}, u32[]{:S(2)}) async-start(bf16[1,64,4,1536]{3,2,0,1:T(4,128)(2,1)} %get-tuple-element.14), calls=%async_computation.1 | async-start | bytes 1572864 | tf_op jit(solution)/shard_map/all_to_all | solution.py:39
  78.9 2.6 %gather_fusion.1 = bf16[512,512]{1,0:T(8,128)(2,1)} fusion(bf16[512,512]{1,0:T(8,128)(2,1)S(1)} %copy-done.1, s32[1024]{0:T(1024)S(1)} %pad_clamp_fusion), kind=kCustom, calls=%fused_computation.1 | custom fusion | bytes 1050624 | tf_op jit(solution)/shard_map/jit(_take)/gather | solution.py:69
  82.8 2.7 %collective-permute-done.1 = bf16[512,1024]{1,0:T(8,128)(2,1)} collective-permute-done((bf16[512,1024]{1,0:T(8,128)(2,1)}, bf16[512,1024]{1,0:T(8,128)(2,1)}, u32[]{:S(2)}, u32[]{:S(2)}) %collective-permute-start.1) | collective-permute-done | bytes 1048608 | tf_op jit(solution)/shard_map/ppermute | solution.py:19
  85.5 2.0 %pad_maximum_fusion = bf16[1536,1024]{1,0:T(8,128)(2,1)S(1)} fusion(bf16[512,1024]{1,0:T(8,128)(2,1)} %collective-permute-done.1, bf16[512,1024]{1,0:T(8,128)(2,1)} %broadcast_select_fusion, bf16[512,1024]{1,0:T(8,128)(2,1)} %collective-permute-done), kind=kLoop, calls=%fused_computation.13 | loop fusion | flops 9437184 | bytes 6291456 | tf_op jit(solution)/shard_map/concatenate | solution.py:15
  87.6 1.9 %fusion.59 = (bf16[1536,512]{1,0:T(8,128)(2,1)}, bf16[1536,512]{1,0:T(8,128)(2,1)}) fusion(bf16[1536,1024]{1,0:T(8,128)(2,1)S(1)} %pad_maximum_fusion), kind=kLoop, calls=%fused_computation.97 | loop fusion | bytes 6291456 | tf_op jit(solution)/shard_map/slice | solution.py:83
  89.4 2.6 %copy.72 = bf16[1536,512]{0,1:T(8,128)(2,1)} copy(bf16[1536,512]{1,0:T(8,128)(2,1)} %get-tuple-element.11) | data formatting | bytes 3145728 | tf_op jit(solution)/shard_map/slice | solution.py:83
  92.0 2.6 %copy.71 = bf16[1536,512]{0,1:T(8,128)(2,1)} copy(bf16[1536,512]{1,0:T(8,128)(2,1)} %get-tuple-element.12) | data formatting | bytes 3145728 | tf_op jit(solution)/shard_map/slice | solution.py:84
  94.6 9.3 %fusion.66 = (f32[4,4,128]{2,0,1:T(4,128)S(1)}, f32[4,4,128,1536]{2,3,0,1:T(8,128)}) fusion(pred[4,1536]{1,0:T(4,128)(4,1)S(1)} %bitcast.116, bf16[1536,4,128,1]{0,2,3,1:T(8,128)(2,1)} %bitcast.115, bf16[4,128,4,128]{3,2,1,0:T(4,128)(2,1)S(1)} %gather.12, pred[4,128]{1,0:T(4,128)(4,1)S(1)} %fusion.72), kind=kOutput, calls=%fused_computation.104 | convolution fusion | flops 818152960 | bytes 14694912 | tf_op jit(solution)/shard_map/sub | solution.py:49
  103.9 2.5 %reshape.183 = bf16[64,4,3,4,128]{4,3,2,1,0:T(4,128)(2,1)} reshape(bf16[1,64,4,1536]{3,2,0,1:T(4,128)(2,1)} %all-to-all-done) | data formatting | bytes 1572864 | tf_op jit(solution)/shard_map/reshape | solution.py:109
  106.4 2.2 %fusion.61 = (bf16[64,4,1,4,128]{4,3,2,1,0:T(4,128)(2,1)}, bf16[64,4,1,4,128]{4,3,2,1,0:T(4,128)(2,1)}, bf16[64,4,1,4,128]{4,3,2,1,0:T(4,128)(2,1)}) fusion(bf16[64,4,3,4,128]{4,3,2,1,0:T(4,128)(2,1)} %reshape.183), kind=kLoop, calls=%fused_computation.99 | loop fusion | bytes 1572864 | tf_op jit(solution)/shard_map/slice | solution.py:125
  108.6 10.9 %all-to-all-done.1 = bf16[1,64,4,1536]{3,2,0,1:T(4,128)(2,1)S(1)} async-done(((bf16[1,64,4,1536]{3,2,0,1:T(4,128)(2,1)}), bf16[1,64,4,1536]{3,2,0,1:T(4,128)(2,1)S(1)}, u32[]{:S(2)}, u32[]{:S(2)}) %all-to-all-start.1) | async-done | bytes 786464 | tf_op jit(solution)/shard_map/all_to_all | solution.py:39
  119.5 1.2 reshape.184
  120.7 1.4 fusion.62
  122.1 1.3 fusion.65
  127.0 28.7 %all-to-all-start.2 = ((bf16[64,1,8,512]{3,2,1,0:T(8,128)(2,1)}), bf16[64,1,8,512]{3,2,1,0:T(8,128)(2,1)}, u32[]{:S(2)}, u32[]{:S(2)}) async-start(bf16[64,1,8,512]{3,2,1,0:T(8,128)(2,1)} %copy.91), calls=%async_computation.2 | async-start | bytes 1048576 | tf_op jit(solution)/shard_map/all_to_all | solution.py:132
  155.8 6.9 %fusion.21 = bf16[4,128,4,128]{1,3,0,2:T(8,128)(2,1)} fusion(bf16[1536,4,128,1]{0,2,3,1:T(8,128)(2,1)} %bitcast.114, f32[4,4,128,1536]{2,3,0,1:T(8,128)} %get-tuple-element.29, f32[4,4,128]{2,0,1:T(4,128)S(1)} %get-tuple-element.28), kind=kOutput, calls=%fused_computation.33 | convolution fusion | flops 811859968 | bytes 14688256 | tf_op jit(solution)/shard_map/jhqk,khd->jqhd/dot_general | solution.py:95
  162.7 2.2 %copy.76 = bf16[4,128,4,128]{3,2,1,0:T(4,128)(2,1)} copy(bf16[4,128,4,128]{1,3,0,2:T(8,128)(2,1)} %fusion.21) | data formatting | bytes 1048576 | tf_op jit(solution)/shard_map/convert_element_type | solution.py:96
  164.9 3.7 %scatter_custom_fusion = bf16[512,512]{1,0:T(8,128)(2,1)} fusion(s32[512]{0:T(512)S(1)} %compare_select_fusion, bf16[64,8,4,128]{3,2,1,0:T(4,128)(2,1)} %bitcast.113, bf16[]{:T(256)} %constant.70.clone.1), kind=kCustom, calls=%fused_computation.47 | custom fusion | bytes 1048578 | tf_op jit(solution)/shard_map/scatter | solution.py:97
  168.5 5.4 %all-to-all-done.2 = bf16[64,1,8,512]{3,2,1,0:T(8,128)(2,1)} async-done(((bf16[64,1,8,512]{3,2,1,0:T(8,128)(2,1)}), bf16[64,1,8,512]{3,2,1,0:T(8,128)(2,1)}, u32[]{:S(2)}, u32[]{:S(2)}) %all-to-all-start.2) | async-done | bytes 524320 | tf_op jit(solution)/shard_map/all_to_all | solution.py:132
  174.0 3.4 %fusion.15 = bf16[1,512,1024]{2,1,0:T(8,128)(2,1)} fusion(bf16[1024,1024]{1,0:T(8,128)(2,1)S(1)} %copy-done, bf16[1,512,1024]{2,1,0:T(8,128)(2,1)S(1)} %copy-done.3, bf16[512,512]{1,0:T(8,128)(2,1)} %bitcast.23, bf16[512,512]{1,0:T(8,128)(2,1)} %scatter_custom_fusion, f32[1024]{0:T(1024)S(1)} %bitcast.117), kind=kOutput, calls=%fused_computation.26 | convolution fusion | flops 1077936128 | bytes 5246976 | tf_op jit(solution)/shard_map/dot_general | solution.py:136
  (46 shorter events, 5.2 us)
Async XLA Ops:
  0.0 173.9 %copy-start = (bf16[1024,1024]{1,0:T(8,128)(2,1)S(1)}, bf16[1024,1024]{1,0:T(8,128)(2,1)}, u32[]{:S(2)}) copy-start(bf16[1024,1024]{1,0:T(8,128)(2,1)} %param.10) | copy-start | bytes 6291460
  0.0 3.3 %copy-start.2 = (bf16[1,512,1024]{2,1,0:T(8,128)(2,1)S(1)}, bf16[1,512,1024]{2,1,0:T(8,128)(2,1)}, u32[]{:S(2)}) copy-start(bf16[1,512,1024]{2,1,0:T(8,128)(2,1)} %param.7) | copy-start | bytes 3145732
  0.0 3.3 %copy-start.6 = (f32[3,1024]{1,0:T(4,128)S(1)}, f32[3,1024]{1,0:T(4,128)}, u32[]{:S(2)}) copy-start(f32[3,1024]{1,0:T(4,128)} %param.8) | copy-start | bytes 36868
  11.3 22.7 %copy-start.5 = (s32[512]{0:T(512)S(1)}, s32[512]{0:T(512)}, u32[]{:S(2)}) copy-start(s32[512]{0:T(512)} %param.11) | copy-start | bytes 6148
  13.0 59.8 %all-to-all-start = ((bf16[1,64,4,1536]{3,2,0,1:T(4,128)(2,1)}), bf16[1,64,4,1536]{3,2,0,1:T(4,128)(2,1)}, u32[]{:S(2)}, u32[]{:S(2)}) async-start(bf16[1,64,4,1536]{3,2,0,1:T(4,128)(2,1)} %get-tuple-element.13), calls=%async_computation | async-start | bytes 1572864 | tf_op jit(solution)/shard_map/all_to_all | solution.py:39
  38.1 6.8 %copy-start.7 = (s32[4,4]{1,0:T(4,128)S(1)}, s32[4,4]{1,0:T(4,128)}, u32[]{:S(2)}) copy-start(s32[4,4]{1,0:T(4,128)} %param.12) | copy-start | bytes 196
  38.1 6.8 %copy-start.8 = (s32[4]{0:T(128)S(1)}, s32[4]{0:T(128)}, u32[]{:S(2)}) copy-start(s32[4]{0:T(128)} %param.13) | copy-start | bytes 52
  38.1 40.7 %copy-start.1 = (bf16[512,512]{1,0:T(8,128)(2,1)S(1)}, bf16[512,512]{1,0:T(8,128)(2,1)}, u32[]{:S(2)}) copy-start(bf16[512,512]{1,0:T(8,128)(2,1)} %get-tuple-element.5) | copy-start | bytes 1572868
  40.6 44.9 %collective-permute-start.1 = (bf16[512,1024]{1,0:T(8,128)(2,1)}, bf16[512,1024]{1,0:T(8,128)(2,1)}, u32[]{:S(2)}, u32[]{:S(2)}) collective-permute-start(bf16[512,1024]{1,0:T(8,128)(2,1)} %broadcast_select_fusion), channel_id=1, source_target_pairs={{64,0},{128,64},{192,128},{256,192},{320,256},{384,320},{448,384},... | collective-permute-start | bytes 3145736 | tf_op jit(solution)/shard_map/ppermute | solution.py:19
  42.5 43.0 %collective-permute-start = (bf16[512,1024]{1,0:T(8,128)(2,1)}, bf16[512,1024]{1,0:T(8,128)(2,1)}, u32[]{:S(2)}, u32[]{:S(2)}) collective-permute-start(bf16[512,1024]{1,0:T(8,128)(2,1)} %broadcast_select_fusion), channel_id=1, source_target_pairs={{0,64},{64,128},{128,192},{192,256},{256,320},{320,384},{384,448},... | collective-permute-start | bytes 3145736 | tf_op jit(solution)/shard_map/ppermute | solution.py:17
  72.8 46.7 %all-to-all-start.1 = ((bf16[1,64,4,1536]{3,2,0,1:T(4,128)(2,1)}), bf16[1,64,4,1536]{3,2,0,1:T(4,128)(2,1)S(1)}, u32[]{:S(2)}, u32[]{:S(2)}) async-start(bf16[1,64,4,1536]{3,2,0,1:T(4,128)(2,1)} %get-tuple-element.14), calls=%async_computation.1 | async-start | bytes 1572864 | tf_op jit(solution)/shard_map/all_to_all | solution.py:39
  120.7 2.9 %copy-start.4 = (bf16[64,4,1,4,128]{4,3,2,1,0:T(4,128)(2,1)S(1)}, bf16[64,4,1,4,128]{4,3,2,1,0:T(4,128)(2,1)}, u32[]{:S(2)}) copy-start(bf16[64,4,1,4,128]{4,3,2,1,0:T(4,128)(2,1)} %get-tuple-element.15) | copy-start | bytes 786436
  127.0 46.9 %all-to-all-start.2 = ((bf16[64,1,8,512]{3,2,1,0:T(8,128)(2,1)}), bf16[64,1,8,512]{3,2,1,0:T(8,128)(2,1)}, u32[]{:S(2)}, u32[]{:S(2)}) async-start(bf16[64,1,8,512]{3,2,1,0:T(8,128)(2,1)} %copy.91), calls=%async_computation.2 | async-start | bytes 1048576 | tf_op jit(solution)/shard_map/all_to_all | solution.py:132
  162.7 11.3 %copy-start.3 = (bf16[1,512,1024]{2,1,0:T(8,128)(2,1)S(1)}, bf16[1,512,1024]{2,1,0:T(8,128)(2,1)}, u32[]{:S(2)}) copy-start(bf16[1,512,1024]{2,1,0:T(8,128)(2,1)} %param.7) | copy-start | bytes 3145732
where the time goes:
time: 178 us; the launch traced here: 177 us
  starting transfers between devices  60.1 us (34%)
  waiting for transfers between devices  46.7 us (26%)
  local copies, waits for them, and re-layouts  31.5 us (18%)
  matrix products  29.2 us (16%)
  other arithmetic  9.71 us (5%)
    all_to_all x2, waiting for transfers between devices, grouped_exchange(): lax.all_to_all(group, axis, split_axis=split_dim, concat_axis=concat_dim,...  38.6 us
    all_to_all x1, starting transfers between devices, body(): lax.all_to_all(mixed_frames, 'frame', split_axis=0, concat_axis=1, tiled=...  28.7 us
    all_to_all x2, starting transfers between devices, grouped_exchange(): lax.all_to_all(group, axis, split_axis=split_dim, concat_axis=concat_dim,...  27 us
    sub x1, matrix products, softmax_last(): expo = jnp.exp(scores - top)  9.27 us
    dot_general x1, matrix products, body(): jnp.einsum('jhqk,khd->jqhd', weights, vals, preferred_element_type=jnp.fl...  6.9 us
    dot_general x1, matrix products, body(): jnp.dot(modulated, w_qkv, preferred_element_type=jnp.float32)  6.72 us
    all_to_all x1, waiting for transfers between devices, body(): lax.all_to_all(mixed_frames, 'frame', split_axis=0, concat_axis=1, tiled=...  5.42 us
    slice x2, local copies, waits for them, and re-layouts, body(): keys = window[:, :half].reshape(3 * tokens, sheads, head_dim)  4.45 us
  transfers between devices with their start and end apart: 5, of which 4 were waited for; matrix products, arithmetic and copies ran while one was open for 26% of the time, Pallas kernels for 0%

commit v1 on v0

v1 whole, which is shorter than its diff:
```python
import jax
import jax.numpy as jnp
from jax import lax
from jax.experimental import pallas as pl
from jax.experimental.pallas import tpu as pltpu
from jax.sharding import Mesh, PartitionSpec as P

HEADS = 8
SHEADS = 4
HD = 128
MAXNB = 4
BLK = 128
NB = 4
CLIP = 8
EPS = 1e-06
NEG = -1e30
F32 = jnp.float32
BF16 = jnp.bfloat16


def dot(a, b):
    return jnp.dot(a, b, preferred_element_type=F32)


def dot_t(a, b):
    return lax.dot_general(a, b, (((1,), (1,)), ((), ())), preferred_element_type=F32)


def modulate(rows, shift, gain):
    mean = jnp.mean(rows, axis=-1, keepdims=True)
    centred = rows - mean
    var = jnp.mean(centred * centred, axis=-1, keepdims=True)
    return (centred * lax.rsqrt(var + EPS) * gain + shift).astype(BF16)


def one_hot_rows(slot_row):
    tokens = slot_row.shape[1]
    cols = jnp.broadcast_to(slot_row, (128, tokens)).T
    lane = lax.broadcasted_iota(jnp.int32, (tokens, 128), 1)
    parts = [
        (cols == lane + 128 * c).astype(F32).astype(BF16) for c in range(tokens // 128)
    ]
    return jnp.concatenate(parts, axis=1)


def spatial_project(x_hbm, cond_ref, slot_ref, w_hbm, kv_hbm, q_hbm, x_s, w_s, mod_s, kv_s, q_s, sem):
    tokens, width = x_s.shape
    half = width // 2
    x_in = pltpu.make_async_copy(x_hbm.at[0], x_s, sem.at[0])
    x_in.start()
    w_in = []
    for i, c in enumerate((width, 2 * width, 0)):
        copy = pltpu.make_async_copy(
            w_hbm.at[:, pl.ds(c, half)], w_s.at[:, pl.ds(i * half, half)], sem.at[1 + i]
        )
        copy.start()
        w_in.append(copy)
    perm = one_hot_rows(slot_ref[...])
    shift = cond_ref[0:1, :]
    gain = 1.0 + cond_ref[1:2, :]
    x_in.wait()
    for j in range(NB):
        sl = slice(j * BLK, (j + 1) * BLK)
        mod_s[sl, :] = modulate(dot(perm[sl, :], x_s[...]), shift, gain)
    outs = []
    for i in range(2):
        w_in[i].wait()
        cs = slice(i * half, (i + 1) * half)
        kv_s[:, cs] = dot(mod_s[...], w_s[:, cs]).astype(BF16)
        out = pltpu.make_async_copy(kv_s.at[:, pl.ds(i * half, half)], kv_hbm.at[:, pl.ds(i * half, half)], sem.at[4 + i])
        out.start()
        outs.append(out)
    w_in[2].wait()
    q_s[...] = dot(mod_s[...], w_s[:, 2 * half :]).astype(BF16)
    out = pltpu.make_async_copy(q_s, q_hbm, sem.at[6])
    out.start()
    outs.append(out)
    for out in outs:
        out.wait()


def temporal(x_hbm, cond_ref, w_hbm, o_ref, x_s, w_s, mod_s, p_s, sem):
    frames, count, width = x_s.shape
    half = width // 2
    rows = frames * count
    x_in = pltpu.make_async_copy(x_hbm, x_s, sem.at[0])
    x_in.start()
    w_in = []
    for i in range(3):
        copy = pltpu.make_async_copy(
            w_hbm.at[:, pl.ds(i * width + half, half)], w_s.at[:, pl.ds(i * half, half)], sem.at[1 + i]
        )
        copy.start()
        w_in.append(copy)
    shift = cond_ref[0:1, :]
    gain = 1.0 + cond_ref[1:2, :]
    x_in.wait()
    for f in range(0, frames, 2):
        piece = x_s[f : f + 2].reshape(2 * count, width).astype(F32)
        mod_s[f * count : (f + 2) * count, :] = modulate(piece, shift, gain)
    for i in range(3):
        w_in[i].wait()
        cs = slice(i * half, (i + 1) * half)
        p_s[:, :, cs] = dot(mod_s[...], w_s[:, cs]).astype(BF16).reshape(frames, count, half)
    group = 128 // frames
    scale = 1.0 / jnp.sqrt(F32(HD))
    ri = lax.broadcasted_iota(jnp.int32, (128, 128), 0) % group
    ci = lax.broadcasted_iota(jnp.int32, (128, 128), 1) % group
    same = ri == ci
    for t in range(count // group):
        ts = slice(t * group, (t + 1) * group)
        for h in range(SHEADS):
            def part(i):
                lo = i * half + h * HD
                return p_s[:, ts, lo : lo + HD].reshape(128, HD)

            s = jnp.where(same, dot_t(part(0), part(1)) * scale, NEG)
            e = jnp.exp(s - jnp.max(s, axis=-1, keepdims=True))
            w = e / jnp.sum(e, axis=-1, keepdims=True)
            hi = w.astype(BF16)
            lo = (w - hi.astype(F32)).astype(BF16)
            v = part(2)
            o = dot(hi, v) + dot(lo, v)
            o_ref[:, ts, h * HD : (h + 1) * HD] = o.astype(BF16).reshape(frames, group, HD)


def finish(nb_ref, cnt_ref, x_hbm, cond_ref, slot_ref, q_hbm, kv_hbm, left_hbm, right_hbm, t_hbm, w_hbm, o_ref,
           x_s, q_s, win, t_s, w_s, blk_s, acc_s, sem):
    tokens, width = x_s.shape
    half = width // 2
    copies = [
        (left_hbm, win.at[pl.ds(0, tokens)]),
        (kv_hbm, win.at[pl.ds(tokens, tokens)]),
        (right_hbm, win.at[pl.ds(2 * tokens, tokens)]),
        (q_hbm, q_s),
        (t_hbm, t_s),
        (w_hbm, w_s),
        (x_hbm.at[0], x_s),
    ]
    copies = [pltpu.make_async_copy(a, b, sem.at[i]) for i, (a, b) in enumerate(copies)]
    for c in copies:
        c.start()
    tok = lax.broadcasted_iota(jnp.int32, (tokens, tokens), 0)
    unperm = (tok == slot_ref[...]).astype(F32).astype(BF16)
    copies[4].wait()
    copies[5].wait()
    acc_s[...] = dot(t_s[...], w_s[half:, :])
    for i in range(4):
        copies[i].wait()
    scale = 1.0 / jnp.sqrt(F32(HD))
    first = nb_ref[0, 0]
    total = 12 * NB
    for j in range(NB):
        rows = slice(j * BLK, (j + 1) * BLK)
        starts = []
        ok = []
        for n in range(MAXNB):
            at = lax.rem(nb_ref[j, n] - first + NB + total, total)
            at = jnp.minimum(at, 3 * NB - 1)
            starts.append(pl.multiple_of(at * BLK, BLK))
            ok.append(n < cnt_ref[j])
        for h in range(SHEADS):
            q = q_s[rows, h * HD : (h + 1) * HD]
            ss = []
            for n in range(MAXNB):
                k = win[pl.ds(starts[n], BLK), h * HD : (h + 1) * HD]
                s = dot_t(q, k) * scale
                if n > 0:
                    s = jnp.where(ok[n], s, NEG)
                ss.append(s)
            top = ss[0]
            for s in ss[1:]:
                top = jnp.maximum(top, s)
            top = jnp.max(top, axis=-1, keepdims=True)
            es = [jnp.exp(s - top) for s in ss]
            tot = jnp.sum(es[0] + es[1] + es[2] + es[3], axis=-1, keepdims=True)
            inv = 1.0 / tot
            o = None
            for n in range(MAXNB):
                v = win[pl.ds(starts[n], BLK), half + h * HD : half + (h + 1) * HD]
                p = dot((es[n] * inv).astype(BF16), v)
                o = p if o is None else o + p
            blk_s[rows, h * HD : (h + 1) * HD] = o.astype(BF16)
    copies[6].wait()
    gate = cond_ref[2:3, :]
    for j in range(NB):
        rows = slice(j * BLK, (j + 1) * BLK)
        sp = dot(unperm[rows, :], blk_s[...]).astype(BF16)
        mixed = dot(sp, w_s[:half, :]) + acc_s[rows, :]
        o_ref[0, rows, :] = (x_s[rows, :].astype(F32) + gate * mixed).astype(BF16)


ANY = pl.BlockSpec(memory_space=pl.ANY)
VM = pl.BlockSpec(memory_space=pltpu.VMEM)
SM = pl.BlockSpec(memory_space=pltpu.SMEM)


def body(latent, cond, w_qkv, w_out, slot, neighbours, counts):
    tokens, width = latent.shape[1], latent.shape[2]
    half = width // 2
    per = tokens // CLIP
    slot_row = slot.reshape(1, tokens)
    seen = lax.all_to_all(latent.reshape(CLIP, per, width), "member", 0, 0, tiled=True)
    kv, q = pl.pallas_call(
        spatial_project,
        out_shape=(
            jax.ShapeDtypeStruct((tokens, width), BF16),
            jax.ShapeDtypeStruct((tokens, half), BF16),
        ),
        in_specs=[ANY, VM, VM, ANY],
        out_specs=(ANY, ANY),
        scratch_shapes=[
            pltpu.VMEM((tokens, width), BF16),
            pltpu.VMEM((width, 3 * half), BF16),
            pltpu.VMEM((tokens, width), BF16),
            pltpu.VMEM((tokens, width), BF16),
            pltpu.VMEM((tokens, half), BF16),
            pltpu.SemaphoreType.DMA((7,)),
        ],
        name="spatial_project",
    )(latent, cond, slot_row, w_qkv)
    count = lax.axis_size("space")
    left = lax.ppermute(kv, "space", [(i, (i + 1) % count) for i in range(count)])
    right = lax.ppermute(kv, "space", [((i + 1) % count, i) for i in range(count)])
    t_out = pl.pallas_call(
        temporal,
        out_shape=jax.ShapeDtypeStruct((CLIP, per, half), BF16),
        in_specs=[ANY, VM, ANY],
        out_specs=VM,
        scratch_shapes=[
            pltpu.VMEM((CLIP, per, width), BF16),
            pltpu.VMEM((width, 3 * half), BF16),
            pltpu.VMEM((tokens, width), BF16),
            pltpu.VMEM((CLIP, per, 3 * half), BF16),
            pltpu.SemaphoreType.DMA((4,)),
        ],
        name="temporal",
    )(seen, cond, w_qkv)
    back = lax.all_to_all(t_out, "member", 0, 0, tiled=True).reshape(tokens, half)
    return pl.pallas_call(
        finish,
        out_shape=jax.ShapeDtypeStruct((1, tokens, width), BF16),
        in_specs=[SM, SM, ANY, VM, VM, ANY, ANY, ANY, ANY, ANY, ANY],
        out_specs=VM,
        scratch_shapes=[
            pltpu.VMEM((tokens, width), BF16),
            pltpu.VMEM((tokens, half), BF16),
            pltpu.VMEM((3 * tokens, width), BF16),
            pltpu.VMEM((tokens, half), BF16),
            pltpu.VMEM((width, width), BF16),
            pltpu.VMEM((tokens, half), BF16),
            pltpu.VMEM((tokens, width), F32),
            pltpu.SemaphoreType.DMA((7,)),
        ],
        name="finish",
    )(neighbours, counts, latent, cond, slot_row, q, kv, left, right, back, w_out)


def solution(mesh):
    devices = mesh.devices
    spaces, frames = devices.shape
    fine = Mesh(devices.reshape(spaces, frames // CLIP, CLIP), ("space", "clip", "member"))
    whole = ("clip", "member")
    in_specs = (P(whole, "space", None), P(), P(), P(), P("space"), P("space", None), P("space"))
    out_specs = P(whole, "space", None)
    return jax.shard_map(body, mesh=fine, in_specs=in_specs, out_specs=out_specs, check_vma=False)
```

time: 178 us -> 63.9 us (0.36)
  the two profiles are of different devices: /device:TPU:136 before, /device:TPU:18 now
where the time goes in v1:
time: 63.9 us; the launch traced here: 63.4 us
  Pallas kernels  26.3 us (41%)
  starting transfers between devices  25.1 us (39%)
  waiting for transfers between devices  9.86 us (15%)
  local copies, waits for them, and re-layouts  2.12 us (3%)
    pallas_call x1, Pallas kernels, body(): pl.pallas_call(finish, out_shape=jax.ShapeDtypeStruct((1, tokens, width),...  13.4 us
    ppermute x1, starting transfers between devices, body(): lax.ppermute(kv, 'space', [((i + 1) % count, i) for i in range(count)])  11.6 us
    ppermute x1, waiting for transfers between devices, body(): lax.ppermute(kv, 'space', [(i, (i + 1) % count) for i in range(count)])  7.41 us
    pallas_call x1, Pallas kernels, body(): pl.pallas_call(temporal, out_shape=jax.ShapeDtypeStruct((CLIP, per, half)...  6.83 us
    pallas_call x1, Pallas kernels, body(): pl.pallas_call(spatial_project, out_shape=(jax.ShapeDtypeStruct((tokens,...  6.07 us
    all_to_all x1, starting transfers between devices, body(): lax.all_to_all(latent.reshape(CLIP, per, width), 'member', 0, 0, tiled=True)  5.84 us
    all_to_all x1, starting transfers between devices, body(): lax.all_to_all(t_out, 'member', 0, 0, tiled=True).reshape(tokens, half)  5.72 us
    ppermute x1, waiting for transfers between devices, body(): lax.ppermute(kv, 'space', [((i + 1) % count, i) for i in range(count)])  2.45 us
  transfers between devices with their start and end apart: 4, of which 2 were waited for; matrix products, arithmetic and copies ran while one was open for 0% of the time, Pallas kernels for 20%

profile of v1, /device:TPU:18, one launch (start us, length us, event | category | flops | bytes accessed | tf_op | source)
XLA Modules:
  0.0 63.4 jit_solution(8325408821202970914)
XLA Ops:
  0.0 5.8 %all-to-all-start = ((bf16[8,64,1024]{2,1,0:T(8,128)(2,1)}), bf16[8,64,1024]{2,1,0:T(8,128)(2,1)S(1)}, u32[]{:S(2)}, u32[]{:S(2)}) async-start(bf16[8,64,1024]{2,1,0:T(8,128)(2,1)} %bitcast.3), calls=%async_computation | async-start | bytes 2097152 | tf_op jit(solution)/shard_map/all_to_all | solution.py:203
  5.8 6.1 %spatial_project.1 = (bf16[512,1024]{1,0:T(8,128)(2,1)}, bf16[512,512]{1,0:T(8,128)(2,1)}) custom-call(bf16[1,512,1024]{2,1,0:T(8,128)(2,1)} %x_hbm.3, f32[3,1024]{1,0:T(4,128)} %cond_ref.5, s32[1,512]{1,0:T(1,128)} %bitcast.5, bf16[1024,3072]{1,0:T(8,128)(2,1)} %w_hbm.4), custom_call_target="tpu_custom_call" | custom-call | tf_op jit(solution)/shard_map/spatial_project/pallas_call | solution.py:204
  11.9 11.6 %collective-permute-start.1 = (bf16[512,1024]{1,0:T(8,128)(2,1)}, bf16[512,1024]{1,0:T(8,128)(2,1)S(1)}, u32[]{:S(2)}, u32[]{:S(2)}) collective-permute-start(bf16[512,1024]{1,0:T(8,128)(2,1)} %get-tuple-element.8.kv_hbm), channel_id=1, source_target_pairs={{64,0},{128,64},{192,128},{256,192},{320,256},{384,320},{448,384},... | collective-permute-start | bytes 3145736 | tf_op jit(solution)/shard_map/ppermute | solution.py:224
  23.5 1.9 %collective-permute-start = (bf16[512,1024]{1,0:T(8,128)(2,1)}, bf16[512,1024]{1,0:T(8,128)(2,1)S(1)}, u32[]{:S(2)}, u32[]{:S(2)}) collective-permute-start(bf16[512,1024]{1,0:T(8,128)(2,1)} %get-tuple-element.8.kv_hbm), channel_id=1, source_target_pairs={{0,64},{64,128},{128,192},{192,256},{256,320},{320,384},{384,448},... | collective-permute-start | bytes 3145736 | tf_op jit(solution)/shard_map/ppermute | solution.py:223
  25.5 0.0 all-to-all-done.x_hbm
  25.5 0.0 copy-start
  25.5 1.0 %copy-done = bf16[8,64,1024]{2,1,0:T(8,128)(2,1)} copy-done((bf16[8,64,1024]{2,1,0:T(8,128)(2,1)}, bf16[8,64,1024]{2,1,0:T(8,128)(2,1)S(1)}, u32[]{:S(2)}) %copy-start) | copy-done | bytes 1048600
  26.4 6.8 %temporal.1 = bf16[8,64,512]{2,1,0:T(8,128)(2,1)} custom-call(bf16[8,64,1024]{2,1,0:T(8,128)(2,1)} %copy-done, f32[3,1024]{1,0:T(4,128)} %cond_ref.5, bf16[1024,3072]{1,0:T(8,128)(2,1)} %w_hbm.4), custom_call_target="tpu_custom_call" | custom-call | tf_op jit(solution)/shard_map/temporal/pallas_call | solution.py:225
  33.3 5.7 %all-to-all-start.1 = ((bf16[8,64,512]{2,1,0:T(8,128)(2,1)}), bf16[8,64,512]{2,1,0:T(8,128)(2,1)S(1)}, u32[]{:S(2)}, u32[]{:S(2)}) async-start(bf16[8,64,512]{2,1,0:T(8,128)(2,1)} %temporal.1), calls=%async_computation.1 | async-start | bytes 1048576 | tf_op jit(solution)/shard_map/all_to_all | solution.py:239
  39.0 2.5 %collective-permute-done.1.right_hbm = bf16[512,1024]{1,0:T(8,128)(2,1)S(1)} collective-permute-done((bf16[512,1024]{1,0:T(8,128)(2,1)}, bf16[512,1024]{1,0:T(8,128)(2,1)S(1)}, u32[]{:S(2)}, u32[]{:S(2)}) %collective-permute-start.1) | collective-permute-done | bytes 1048608 | tf_op jit(solution)/shard_map/ppermute | solution.py:224
  41.5 0.0 copy-start.2
  41.5 7.4 %collective-permute-done.left_hbm = bf16[512,1024]{1,0:T(8,128)(2,1)S(1)} collective-permute-done((bf16[512,1024]{1,0:T(8,128)(2,1)}, bf16[512,1024]{1,0:T(8,128)(2,1)S(1)}, u32[]{:S(2)}, u32[]{:S(2)}) %collective-permute-start) | collective-permute-done | bytes 1048608 | tf_op jit(solution)/shard_map/ppermute | solution.py:223
  48.9 0.0 copy-start.3
  48.9 0.0 all-to-all-done.1
  48.9 0.0 copy-start.1
  48.9 0.0 copy-done.2
  48.9 1.0 %copy-done.3 = bf16[512,1024]{1,0:T(8,128)(2,1)} copy-done((bf16[512,1024]{1,0:T(8,128)(2,1)}, bf16[512,1024]{1,0:T(8,128)(2,1)S(1)}, u32[]{:S(2)}) %copy-start.3) | copy-done | bytes 1048600
  49.9 0.1 copy-done.1
  50.0 13.4 %finish.1 = bf16[1,512,1024]{2,1,0:T(8,128)(2,1)} custom-call(s32[4,4]{1,0:T(4,128)} %nb_ref.1, s32[4]{0:T(128)} %cnt_ref.1, bf16[1,512,1024]{2,1,0:T(8,128)(2,1)} %x_hbm.3, f32[3,1024]{1,0:T(4,128)} %cond_ref.5, s32[1,512]{1,0:T(1,128)} %bitcast.6, bf16[512,512]{1,0:T(8,128)(2,1)} %get-tuple-element.7.q_hbm, bf16[512,1024]{1,0:T(8,128)(2,1)} %get-tuple-element.8.kv_hbm, ...), custom_call_target="tpu_custom_call" | custom-call | tf_op jit(solution)/shard_map/finish/pallas_call | solution.py:240
Async XLA Ops:
  0.0 25.5 %all-to-all-start = ((bf16[8,64,1024]{2,1,0:T(8,128)(2,1)}), bf16[8,64,1024]{2,1,0:T(8,128)(2,1)S(1)}, u32[]{:S(2)}, u32[]{:S(2)}) async-start(bf16[8,64,1024]{2,1,0:T(8,128)(2,1)} %bitcast.3), calls=%async_computation | async-start | bytes 2097152 | tf_op jit(solution)/shard_map/all_to_all | solution.py:203
  11.9 29.5 %collective-permute-start.1 = (bf16[512,1024]{1,0:T(8,128)(2,1)}, bf16[512,1024]{1,0:T(8,128)(2,1)S(1)}, u32[]{:S(2)}, u32[]{:S(2)}) collective-permute-start(bf16[512,1024]{1,0:T(8,128)(2,1)} %get-tuple-element.8.kv_hbm), channel_id=1, source_target_pairs={{64,0},{128,64},{192,128},{256,192},{320,256},{384,320},{448,384},... | collective-permute-start | bytes 3145736 | tf_op jit(solution)/shard_map/ppermute | solution.py:224
  23.5 25.3 %collective-permute-start = (bf16[512,1024]{1,0:T(8,128)(2,1)}, bf16[512,1024]{1,0:T(8,128)(2,1)S(1)}, u32[]{:S(2)}, u32[]{:S(2)}) collective-permute-start(bf16[512,1024]{1,0:T(8,128)(2,1)} %get-tuple-element.8.kv_hbm), channel_id=1, source_target_pairs={{0,64},{64,128},{128,192},{192,256},{256,320},{320,384},{384,448},... | collective-permute-start | bytes 3145736 | tf_op jit(solution)/shard_map/ppermute | solution.py:223
  25.5 1.0 %copy-start = (bf16[8,64,1024]{2,1,0:T(8,128)(2,1)}, bf16[8,64,1024]{2,1,0:T(8,128)(2,1)S(1)}, u32[]{:S(2)}) copy-start(bf16[8,64,1024]{2,1,0:T(8,128)(2,1)S(1)} %all-to-all-done.x_hbm) | copy-start | bytes 3145732
  33.3 15.6 %all-to-all-start.1 = ((bf16[8,64,512]{2,1,0:T(8,128)(2,1)}), bf16[8,64,512]{2,1,0:T(8,128)(2,1)S(1)}, u32[]{:S(2)}, u32[]{:S(2)}) async-start(bf16[8,64,512]{2,1,0:T(8,128)(2,1)} %temporal.1), calls=%async_computation.1 | async-start | bytes 1048576 | tf_op jit(solution)/shard_map/all_to_all | solution.py:239
  41.5 7.4 %copy-start.2 = (bf16[512,1024]{1,0:T(8,128)(2,1)}, bf16[512,1024]{1,0:T(8,128)(2,1)S(1)}, u32[]{:S(2)}) copy-start(bf16[512,1024]{1,0:T(8,128)(2,1)S(1)} %collective-permute-done.1.right_hbm) | copy-start | bytes 3145732
  48.9 1.0 %copy-start.3 = (bf16[512,1024]{1,0:T(8,128)(2,1)}, bf16[512,1024]{1,0:T(8,128)(2,1)S(1)}, u32[]{:S(2)}) copy-start(bf16[512,1024]{1,0:T(8,128)(2,1)S(1)} %collective-permute-done.left_hbm) | copy-start | bytes 3145732
  48.9 1.2 %copy-start.1 = (bf16[8,64,512]{2,1,0:T(8,128)(2,1)}, bf16[8,64,512]{2,1,0:T(8,128)(2,1)S(1)}, u32[]{:S(2)}) copy-start(bf16[8,64,512]{2,1,0:T(8,128)(2,1)S(1)} %all-to-all-done.1) | copy-start | bytes 1572868

commit v2 on v1

v2 whole, which is shorter than its diff:
```python
import jax
import jax.numpy as jnp
from jax import lax
from jax.experimental import pallas as pl
from jax.experimental.pallas import tpu as pltpu
from jax.sharding import Mesh, PartitionSpec as P

HEADS = 8
SHEADS = 4
HD = 128
MAXNB = 4
BLK = 128
NB = 4
CLIP = 8
EPS = 1e-06
NEG = -1e30
F32 = jnp.float32
BF16 = jnp.bfloat16


def dot(a, b):
    return jnp.dot(a, b, preferred_element_type=F32)


def dot_t(a, b):
    return lax.dot_general(a, b, (((1,), (1,)), ((), ())), preferred_element_type=F32)


def modulate(rows, shift, gain):
    mean = jnp.mean(rows, axis=-1, keepdims=True)
    centred = rows - mean
    var = jnp.mean(centred * centred, axis=-1, keepdims=True)
    return (centred * lax.rsqrt(var + EPS) * gain + shift).astype(BF16)


def one_hot_rows(slot_row):
    tokens = slot_row.shape[1]
    cols = jnp.broadcast_to(slot_row, (128, tokens)).T
    lane = lax.broadcasted_iota(jnp.int32, (tokens, 128), 1)
    parts = [
        (cols == lane + 128 * c).astype(F32).astype(BF16) for c in range(tokens // 128)
    ]
    return jnp.concatenate(parts, axis=1)


def spatial_keyval(x_hbm, cond_ref, slot_ref, w_hbm, kv_hbm, mod_hbm, x_s, w_s, mod_s, kv_s, sem):
    tokens, width = x_s.shape
    half = width // 2
    x_in = pltpu.make_async_copy(x_hbm.at[0], x_s, sem.at[5])
    x_in.start()
    halves = [slice(i * half, (i + 1) * half) for i in range(2)]
    w_in = []
    for i, cs in enumerate(halves):
        copy = pltpu.make_async_copy(w_hbm.at[:, pl.ds((i + 1) * width, half)], w_s.at[:, cs], sem.at[i])
        copy.start()
        w_in.append(copy)
    perm = one_hot_rows(slot_ref[...])
    shift = cond_ref[0:1, :]
    gain = 1.0 + cond_ref[1:2, :]
    x_in.wait()
    for j in range(NB):
        sl = slice(j * BLK, (j + 1) * BLK)
        mod_s[sl, :] = modulate(dot(perm[sl, :], x_s[...]), shift, gain)
    outs = [pltpu.make_async_copy(mod_s, mod_hbm, sem.at[2])]
    outs[0].start()
    for i, cs in enumerate(halves):
        w_in[i].wait()
        kv_s[:, cs] = dot(mod_s[...], w_s[:, cs]).astype(BF16)
        out = pltpu.make_async_copy(kv_s.at[:, cs], kv_hbm.at[:, cs], sem.at[3 + i])
        out.start()
        outs.append(out)
    for out in outs:
        out.wait()


def spatial_query(mod_hbm, w_hbm, q_ref, mod_s, w_s, sem):
    half = q_ref.shape[1]
    w_in = pltpu.make_async_copy(w_hbm.at[:, pl.ds(0, half)], w_s, sem.at[0])
    m_in = pltpu.make_async_copy(mod_hbm, mod_s, sem.at[1])
    w_in.start()
    m_in.start()
    w_in.wait()
    m_in.wait()
    q_ref[...] = dot(mod_s[...], w_s[...]).astype(BF16)


def temporal(x_ref, cond_ref, w_hbm, o_hbm, w_s, mod_s, p_s, o_s, sem):
    frames, count, width = x_ref.shape
    half = width // 2
    w_in = []
    for i in range(3):
        copy = pltpu.make_async_copy(
            w_hbm.at[:, pl.ds(i * width + half, half)], w_s.at[:, pl.ds(i * half, half)], sem.at[i]
        )
        copy.start()
        w_in.append(copy)
    shift = cond_ref[0:1, :]
    gain = 1.0 + cond_ref[1:2, :]
    for f in range(0, frames, 2):
        piece = x_ref[f : f + 2].reshape(2 * count, width).astype(F32)
        mod_s[f * count : (f + 2) * count, :] = modulate(piece, shift, gain)
    for i in range(3):
        w_in[i].wait()
        cs = slice(i * half, (i + 1) * half)
        p_s[:, :, cs] = dot(mod_s[...], w_s[:, cs]).astype(BF16).reshape(frames, count, half)
    group = 128 // frames
    scale = 1.0 / jnp.sqrt(F32(HD))
    ri = lax.broadcasted_iota(jnp.int32, (128, 128), 0) % group
    ci = lax.broadcasted_iota(jnp.int32, (128, 128), 1) % group
    same = ri == ci
    outs = []
    for t in range(count // group):
        ts = slice(t * group, (t + 1) * group)

        def part(i, h):
            lo = i * half + h * HD
            return p_s[:, ts, lo : lo + HD].reshape(128, HD)

        heads = range(SHEADS)
        ss = [jnp.where(same, dot_t(part(0, h), part(1, h)) * scale, NEG) for h in heads]
        es = [jnp.exp(s - jnp.max(s, axis=-1, keepdims=True)) for s in ss]
        ws = [e * (1.0 / jnp.sum(e, axis=-1, keepdims=True)) for e in es]
        his = [w.astype(BF16) for w in ws]
        los = [(w - hi.astype(F32)).astype(BF16) for w, hi in zip(ws, his)]
        for h in heads:
            o = dot(his[h], part(2, h)) + dot(los[h], part(2, h))
            o_s[:, ts, h * HD : (h + 1) * HD] = o.astype(BF16).reshape(frames, group, HD)
        out = pltpu.make_async_copy(o_s.at[:, ts], o_hbm.at[:, ts], sem.at[3 + t])
        out.start()
        outs.append(out)
    for out in outs:
        out.wait()


def finish(nb_ref, cnt_ref, x_hbm, cond_ref, slot_ref, q_hbm, kv_hbm, left_hbm, right_hbm, t_ref, w_ref, o_hbm,
           x_s, q_ref, win, blk_s, acc_s, o_s, sem):
    tokens, width = x_s.shape
    half = width // 2
    copies = [
        (left_hbm, win.at[pl.ds(0, tokens)]),
        (right_hbm, win.at[pl.ds(2 * tokens, tokens)]),
        (kv_hbm, win.at[pl.ds(tokens, tokens)]),
        (q_hbm, q_ref),
        (x_hbm.at[0], x_s),
    ]
    copies = [pltpu.make_async_copy(a, b, sem.at[i]) for i, (a, b) in enumerate(copies)]
    for c in copies:
        c.start()
    tok = lax.broadcasted_iota(jnp.int32, (tokens, tokens), 0)
    unperm = (tok == slot_ref[...]).astype(F32).astype(BF16)
    acc_s[...] = dot(t_ref[...], w_ref[half:, :])
    scale = 1.0 / jnp.sqrt(F32(HD))
    first = nb_ref[0, 0]
    total = 12 * NB
    for c in copies[:4]:
        c.wait()
    for j in range(NB):
        rows = slice(j * BLK, (j + 1) * BLK)
        starts = []
        lane = lax.broadcasted_iota(jnp.int32, (BLK, MAXNB * BLK), 1)
        keep = lane < cnt_ref[j] * BLK
        for n in range(MAXNB):
            at = lax.rem(nb_ref[j, n] - first + NB + total, total)
            at = jnp.minimum(at, 3 * NB - 1)
            starts.append(pl.multiple_of(at * BLK, BLK))

        def listed(lo):
            return jnp.concatenate([win[pl.ds(at, BLK), lo : lo + HD] for at in starts], axis=0)

        heads = range(SHEADS)
        cols = [slice(h * HD, (h + 1) * HD) for h in heads]
        ss = [jnp.where(keep, dot_t(q_ref[rows, cols[h]], listed(h * HD)) * scale, NEG) for h in heads]
        tops = [jnp.max(s, axis=-1, keepdims=True) for s in ss]
        es = [jnp.exp(s - top) for s, top in zip(ss, tops)]
        invs = [1.0 / jnp.sum(e, axis=-1, keepdims=True) for e in es]
        ps = [(e * inv).astype(BF16) for e, inv in zip(es, invs)]
        for h in heads:
            blk_s[rows, cols[h]] = dot(ps[h], listed(half + h * HD)).astype(BF16)
    copies[4].wait()
    gate = cond_ref[2:3, :]
    outs = []
    for j in range(NB):
        rows = slice(j * BLK, (j + 1) * BLK)
        sp = dot(unperm[rows, :], blk_s[...]).astype(BF16)
        mixed = dot(sp, w_ref[:half, :]) + acc_s[rows, :]
        o_s[rows, :] = (x_s[rows, :].astype(F32) + gate * mixed).astype(BF16)
        out = pltpu.make_async_copy(o_s.at[rows], o_hbm.at[0, rows], sem.at[5 + j])
        out.start()
        outs.append(out)
    for out in outs:
        out.wait()


HB = pl.BlockSpec(memory_space=pltpu.HBM)
VM = pl.BlockSpec(memory_space=pltpu.VMEM)
SM = pl.BlockSpec(memory_space=pltpu.SMEM)
DMA = pltpu.SemaphoreType.DMA


def near(x):
    return pltpu.with_memory_space_constraint(x, pltpu.VMEM)


def call(kernel, ins, outs, shapes, scratch):
    return pl.pallas_call(
        kernel,
        out_shape=shapes,
        in_specs=ins,
        out_specs=outs,
        scratch_shapes=scratch,
        name=kernel.__name__,
    )


def body(latent, cond, w_qkv, w_out, slot, neighbours, counts):
    tokens, width = latent.shape[1], latent.shape[2]
    half = width // 2
    per = tokens // CLIP
    slot_row = slot.reshape(1, tokens)
    arr = jax.ShapeDtypeStruct
    room = lambda *shape: pltpu.VMEM(shape, BF16)
    seen = lax.all_to_all(latent.reshape(CLIP, per, width), "member", 0, 0, tiled=True)
    kv, mod = call(
        spatial_keyval,
        [HB, VM, VM, HB],
        (HB, HB),
        (arr((tokens, width), BF16), arr((tokens, width), BF16)),
        [room(tokens, width), room(width, width), room(tokens, width), room(tokens, width), DMA((6,))],
    )(latent, cond, slot_row, w_qkv)
    count = lax.axis_size("space")
    left = lax.ppermute(kv, "space", [(i, (i + 1) % count) for i in range(count)])
    right = lax.ppermute(kv, "space", [((i + 1) % count, i) for i in range(count)])
    q = call(
        spatial_query,
        [HB, HB],
        VM,
        arr((tokens, half), BF16),
        [room(tokens, width), room(width, half), DMA((2,))],
    )(mod, w_qkv)
    t_out = call(
        temporal,
        [VM, VM, HB],
        HB,
        arr((CLIP, per, half), BF16),
        [
            room(width, 3 * half),
            room(tokens, width),
            room(CLIP, per, 3 * half),
            room(CLIP, per, half),
            DMA((3 + per // (128 // CLIP),)),
        ],
    )(near(seen), cond, w_qkv)
    back = lax.all_to_all(t_out, "member", 0, 0, tiled=True).reshape(tokens, half)
    return call(
        finish,
        [SM, SM, HB, VM, VM, HB, HB, HB, HB, VM, VM],
        HB,
        arr((1, tokens, width), BF16),
        [
            room(tokens, width),
            room(tokens, half),
            room(3 * tokens, width),
            room(tokens, half),
            pltpu.VMEM((tokens, width), F32),
            room(tokens, width),
            DMA((9,)),
        ],
    )(neighbours, counts, latent, cond, slot_row, q, kv, left, right, near(back), near(w_out))


def solution(mesh):
    devices = mesh.devices
    spaces, frames = devices.shape
    fine = Mesh(devices.reshape(spaces, frames // CLIP, CLIP), ("space", "clip", "member"))
    whole = ("clip", "member")
    in_specs = (P(whole, "space", None), P(), P(), P(), P("space"), P("space", None), P("space"))
    out_specs = P(whole, "space", None)
    return jax.shard_map(body, mesh=fine, in_specs=in_specs, out_specs=out_specs, check_vma=False)
```

time: 63.9 us -> 56.4 us (0.88)
  Pallas kernels: 26.3 us -> 22.7 us
  local copies, waits for them, and re-layouts: 2.12 us -> 0.01 us
  waiting for transfers between devices: 9.86 us -> 7.97 us
    pallas_call x3 -> x4, Pallas kernels: 26.3 us -> 22.7 us  [the longest x1 7.63 us: body(): call(finish, [SM, SM, HB, VM, VM, HB, HB, HB, HB, VM, VM], HB, arr((1, to...]
    unnamed x8 -> x2, local copies, waits for them, and re-layouts: 2.12 us -> 0.01 us
    ppermute x1, waiting for transfers between devices: 2.45 us -> 0.46 us  [body(): lax.ppermute(kv, 'space', [((i + 1) % count, i) for i in range(count)])]
  transfers between devices with their start and end apart: 4 -> 4, of which waited for: 2 -> 2; matrix products, arithmetic and copies ran while one was open for 0% -> 0% of each run, Pallas kernels for 20% -> 27%
where the time goes in v2:
time: 56.4 us; the launch traced here: 55.9 us
  starting transfers between devices  25.2 us (45%)
  Pallas kernels  22.7 us (40%)
  waiting for transfers between devices  7.97 us (14%)
    ppermute x1, starting transfers between devices, body(): lax.ppermute(kv, 'space', [((i + 1) % count, i) for i in range(count)])  11.6 us
    pallas_call x1, Pallas kernels, body(): call(finish, [SM, SM, HB, VM, VM, HB, HB, HB, HB, VM, VM], HB, arr((1, to...  7.63 us
    ppermute x1, waiting for transfers between devices, body(): lax.ppermute(kv, 'space', [(i, (i + 1) % count) for i in range(count)])  7.51 us
    pallas_call x1, Pallas kernels, body(): call(temporal, [VM, VM, HB], HB, arr((CLIP, per, half), BF16), [room(widt...  6.6 us
    all_to_all x1, starting transfers between devices, body(): lax.all_to_all(latent.reshape(CLIP, per, width), 'member', 0, 0, tiled=True)  5.84 us
    all_to_all x1, starting transfers between devices, body(): lax.all_to_all(t_out, 'member', 0, 0, tiled=True).reshape(tokens, half)  5.84 us
    pallas_call x1, Pallas kernels, body(): call(spatial_keyval, [HB, VM, VM, HB], (HB, HB), (arr((tokens, width), BF...  5.42 us
    pallas_call x1, Pallas kernels, body(): call(spatial_query, [HB, HB], VM, arr((tokens, half), BF16), [room(tokens...  3.06 us
  transfers between devices with their start and end apart: 4, of which 2 were waited for; matrix products, arithmetic and copies ran while one was open for 0% of the time, Pallas kernels for 27%

profile of v2, /device:TPU:18, one launch (start us, length us, event | category | flops | bytes accessed | tf_op | source)
XLA Modules:
  0.0 55.9 jit_solution(1189039957448301962)
XLA Ops:
  0.0 5.8 %all-to-all-start = ((bf16[8,64,1024]{2,1,0:T(8,128)(2,1)}), bf16[8,64,1024]{2,1,0:T(8,128)(2,1)S(1)}, u32[]{:S(2)}, u32[]{:S(2)}) async-start(bf16[8,64,1024]{2,1,0:T(8,128)(2,1)} %bitcast.4), calls=%async_computation | async-start | bytes 2097152 | tf_op jit(solution)/shard_map/all_to_all | solution.py:222
  5.8 5.4 %spatial_keyval.1 = (bf16[512,1024]{1,0:T(8,128)(2,1)}, bf16[512,1024]{1,0:T(8,128)(2,1)}) custom-call(bf16[1,512,1024]{2,1,0:T(8,128)(2,1)} %x_hbm.3, f32[3,1024]{1,0:T(4,128)} %cond_ref.5, s32[1,512]{1,0:T(1,128)} %bitcast.5, bf16[1024,3072]{1,0:T(8,128)(2,1)} %w_hbm.5), custom_call_target="tpu_custom_call" | custom-call | tf_op jit(solution)/shard_map/spatial_keyval/pallas_call | solution.py:223
  11.3 11.6 %collective-permute-start.1 = (bf16[512,1024]{1,0:T(8,128)(2,1)}, bf16[512,1024]{1,0:T(8,128)(2,1)}, u32[]{:S(2)}, u32[]{:S(2)}) collective-permute-start(bf16[512,1024]{1,0:T(8,128)(2,1)} %get-tuple-element.8.kv_hbm), channel_id=1, source_target_pairs={{64,0},{128,64},{192,128},{256,192},{320,256},{384,320},{448,384},... | collective-permute-start | bytes 3145736 | tf_op jit(solution)/shard_map/ppermute | solution.py:232
  22.9 1.9 %collective-permute-start = (bf16[512,1024]{1,0:T(8,128)(2,1)}, bf16[512,1024]{1,0:T(8,128)(2,1)}, u32[]{:S(2)}, u32[]{:S(2)}) collective-permute-start(bf16[512,1024]{1,0:T(8,128)(2,1)} %get-tuple-element.8.kv_hbm), channel_id=1, source_target_pairs={{0,64},{64,128},{128,192},{192,256},{256,320},{320,384},{384,448},... | collective-permute-start | bytes 3145736 | tf_op jit(solution)/shard_map/ppermute | solution.py:231
  24.8 0.0 all-to-all-done.x_ref
  24.8 6.6 %temporal.1 = bf16[8,64,512]{2,1,0:T(8,128)(2,1)} custom-call(bf16[8,64,1024]{2,1,0:T(8,128)(2,1)S(1)} %all-to-all-done.x_ref, f32[3,1024]{1,0:T(4,128)} %cond_ref.5, bf16[1024,3072]{1,0:T(8,128)(2,1)} %w_hbm.5), custom_call_target="tpu_custom_call" | custom-call | tf_op jit(solution)/shard_map/temporal/pallas_call | solution.py:240
  31.4 0.0 copy-start
  31.4 5.8 %all-to-all-start.1 = ((bf16[8,64,512]{2,1,0:T(8,128)(2,1)}), bf16[8,64,512]{2,1,0:T(8,128)(2,1)S(1)}, u32[]{:S(2)}, u32[]{:S(2)}) async-start(bf16[8,64,512]{2,1,0:T(8,128)(2,1)} %temporal.1), calls=%async_computation.1 | async-start | bytes 1048576 | tf_op jit(solution)/shard_map/all_to_all | solution.py:253
  37.3 3.1 %spatial_query.1.q_hbm = bf16[512,512]{1,0:T(8,128)(2,1)} custom-call(bf16[512,1024]{1,0:T(8,128)(2,1)} %get-tuple-element.7.mod_hbm, bf16[1024,3072]{1,0:T(8,128)(2,1)} %w_hbm.5), custom_call_target="tpu_custom_call" | custom-call | tf_op jit(solution)/shard_map/spatial_query/pallas_call | solution.py:233
  40.4 0.5 collective-permute-done.1.right_hbm
  40.8 7.5 %collective-permute-done.left_hbm = bf16[512,1024]{1,0:T(8,128)(2,1)} collective-permute-done((bf16[512,1024]{1,0:T(8,128)(2,1)}, bf16[512,1024]{1,0:T(8,128)(2,1)}, u32[]{:S(2)}, u32[]{:S(2)}) %collective-permute-start) | collective-permute-done | bytes 1048608 | tf_op jit(solution)/shard_map/ppermute | solution.py:231
  48.3 0.0 all-to-all-done.1
  48.3 0.0 copy-done
  48.3 7.6 %finish.1 = bf16[1,512,1024]{2,1,0:T(8,128)(2,1)} custom-call(s32[4,4]{1,0:T(4,128)} %nb_ref.1, s32[4]{0:T(128)} %cnt_ref.1, bf16[1,512,1024]{2,1,0:T(8,128)(2,1)} %x_hbm.3, f32[3,1024]{1,0:T(4,128)} %cond_ref.5, s32[1,512]{1,0:T(1,128)} %bitcast.6, bf16[512,512]{1,0:T(8,128)(2,1)} %spatial_query.1.q_hbm, bf16[512,1024]{1,0:T(8,128)(2,1)} %get-tuple-element.8.kv_hbm, ...), custom_call_target="tpu_custom_call" | custom-call | tf_op jit(solution)/shard_map/finish/pallas_call | solution.py:254
Async XLA Ops:
  0.0 24.8 %all-to-all-start = ((bf16[8,64,1024]{2,1,0:T(8,128)(2,1)}), bf16[8,64,1024]{2,1,0:T(8,128)(2,1)S(1)}, u32[]{:S(2)}, u32[]{:S(2)}) async-start(bf16[8,64,1024]{2,1,0:T(8,128)(2,1)} %bitcast.4), calls=%async_computation | async-start | bytes 2097152 | tf_op jit(solution)/shard_map/all_to_all | solution.py:222
  11.3 29.5 %collective-permute-start.1 = (bf16[512,1024]{1,0:T(8,128)(2,1)}, bf16[512,1024]{1,0:T(8,128)(2,1)}, u32[]{:S(2)}, u32[]{:S(2)}) collective-permute-start(bf16[512,1024]{1,0:T(8,128)(2,1)} %get-tuple-element.8.kv_hbm), channel_id=1, source_target_pairs={{64,0},{128,64},{192,128},{256,192},{320,256},{384,320},{448,384},... | collective-permute-start | bytes 3145736 | tf_op jit(solution)/shard_map/ppermute | solution.py:232
  22.9 25.4 %collective-permute-start = (bf16[512,1024]{1,0:T(8,128)(2,1)}, bf16[512,1024]{1,0:T(8,128)(2,1)}, u32[]{:S(2)}, u32[]{:S(2)}) collective-permute-start(bf16[512,1024]{1,0:T(8,128)(2,1)} %get-tuple-element.8.kv_hbm), channel_id=1, source_target_pairs={{0,64},{64,128},{128,192},{192,256},{256,320},{320,384},{384,448},... | collective-permute-start | bytes 3145736 | tf_op jit(solution)/shard_map/ppermute | solution.py:231
  31.4 16.9 %copy-start = (bf16[1024,1024]{1,0:T(8,128)(2,1)S(1)}, bf16[1024,1024]{1,0:T(8,128)(2,1)}, u32[]{:S(2)}) copy-start(bf16[1024,1024]{1,0:T(8,128)(2,1)} %w_ref.1) | copy-start | bytes 6291460
  31.4 16.9 %all-to-all-start.1 = ((bf16[8,64,512]{2,1,0:T(8,128)(2,1)}), bf16[8,64,512]{2,1,0:T(8,128)(2,1)S(1)}, u32[]{:S(2)}, u32[]{:S(2)}) async-start(bf16[8,64,512]{2,1,0:T(8,128)(2,1)} %temporal.1), calls=%async_computation.1 | async-start | bytes 1048576 | tf_op jit(solution)/shard_map/all_to_all | solution.py:253

commit v3 on v2

--- a/solution.py
+++ b/solution.py
@@ -13,7 +13,8 @@
 NB = 4
 CLIP = 8
 EPS = 1e-06
-NEG = -1e30
+NEG = -jnp.inf
+LOG2E = 1.4426950408889634
 F32 = jnp.float32
 BF16 = jnp.bfloat16
 
@@ -43,28 +44,37 @@
     return jnp.concatenate(parts, axis=1)
 
 
-def spatial_keyval(x_hbm, cond_ref, slot_ref, w_hbm, kv_hbm, mod_hbm, x_s, w_s, mod_s, kv_s, sem):
+def spatial_keyval(x_hbm, cond_hbm, slot_hbm, w_hbm, kv_hbm, mod_hbm, cond_ref, slot_ref, x_s, w_s, mod_s, kv_s, sem):
     tokens, width = x_s.shape
     half = width // 2
-    x_in = pltpu.make_async_copy(x_hbm.at[0], x_s, sem.at[5])
+    x_in = pltpu.make_async_copy(x_hbm.at[0], x_s, sem.at[7])
+    s_in = pltpu.make_async_copy(slot_hbm, slot_ref, sem.at[8])
+    c_in = pltpu.make_async_copy(cond_hbm, cond_ref, sem.at[9])
+    s_in.start()
     x_in.start()
-    halves = [slice(i * half, (i + 1) * half) for i in range(2)]
+    c_in.start()
+    s_in.wait()
+    perm = one_hot_rows(slot_ref[...])
+    x_in.wait()
+    c_in.wait()
+    shift = cond_ref[0:1, :]
+    gain = 1.0 + cond_ref[1:2, :]
     w_in = []
-    for i, cs in enumerate(halves):
+    for i in range(2):
+        cs = slice(i * half, (i + 1) * half)
         copy = pltpu.make_async_copy(w_hbm.at[:, pl.ds((i + 1) * width, half)], w_s.at[:, cs], sem.at[i])
         copy.start()
         w_in.append(copy)
-    perm = one_hot_rows(slot_ref[...])
-    shift = cond_ref[0:1, :]
-    gain = 1.0 + cond_ref[1:2, :]
-    x_in.wait()
     for j in range(NB):
         sl = slice(j * BLK, (j + 1) * BLK)
         mod_s[sl, :] = modulate(dot(perm[sl, :], x_s[...]), shift, gain)
     outs = [pltpu.make_async_copy(mod_s, mod_hbm, sem.at[2])]
     outs[0].start()
-    for i, cs in enumerate(halves):
-        w_in[i].wait()
+    quarter = half // 2
+    for i in range(4):
+        if i % 2 == 0:
+            w_in[i // 2].wait()
+        cs = slice(i * quarter, (i + 1) * quarter)
         kv_s[:, cs] = dot(mod_s[...], w_s[:, cs]).astype(BF16)
         out = pltpu.make_async_copy(kv_s.at[:, cs], kv_hbm.at[:, cs], sem.at[3 + i])
         out.start()
@@ -84,9 +94,11 @@
     q_ref[...] = dot(mod_s[...], w_s[...]).astype(BF16)
 
 
-def temporal(x_ref, cond_ref, w_hbm, o_hbm, w_s, mod_s, p_s, o_s, sem):
+def temporal(x_ref, cond_hbm, w_hbm, o_hbm, cond_ref, w_s, mod_s, p_s, o_s, sem):
     frames, count, width = x_ref.shape
     half = width // 2
+    c_in = pltpu.make_async_copy(cond_hbm, cond_ref, sem.at[7])
+    c_in.start()
     w_in = []
     for i in range(3):
         copy = pltpu.make_async_copy(
@@ -94,6 +106,7 @@
         )
         copy.start()
         w_in.append(copy)
+    c_in.wait()
     shift = cond_ref[0:1, :]
     gain = 1.0 + cond_ref[1:2, :]
     for f in range(0, frames, 2):
@@ -132,8 +145,8 @@
         out.wait()
 
 
-def finish(nb_ref, cnt_ref, x_hbm, cond_ref, slot_ref, q_hbm, kv_hbm, left_hbm, right_hbm, t_ref, w_ref, o_hbm,
-           x_s, q_ref, win, blk_s, acc_s, o_s, sem):
+def finish(nb_hbm, cnt_hbm, x_hbm, cond_hbm, slot_hbm, q_hbm, kv_hbm, left_hbm, right_hbm, t_ref, w_ref, o_hbm,
+           nb_ref, cnt_ref, cond_ref, slot_ref, x_s, q_ref, win, blk_s, acc_s, o_s, sem):
     tokens, width = x_s.shape
     half = width // 2
     copies = [
@@ -141,21 +154,27 @@
         (right_hbm, win.at[pl.ds(2 * tokens, tokens)]),
         (kv_hbm, win.at[pl.ds(tokens, tokens)]),
         (q_hbm, q_ref),
+        (slot_hbm, slot_ref),
+        (nb_hbm, nb_ref),
+        (cnt_hbm, cnt_ref),
+        (cond_hbm, cond_ref),
         (x_hbm.at[0], x_s),
     ]
     copies = [pltpu.make_async_copy(a, b, sem.at[i]) for i, (a, b) in enumerate(copies)]
-    for c in copies:
+    for c in copies[4:8] + copies[:4]:
         c.start()
+    acc_s[...] = dot(t_ref[...], w_ref[half:, :])
+    copies[4].wait()
     tok = lax.broadcasted_iota(jnp.int32, (tokens, tokens), 0)
     unperm = (tok == slot_ref[...]).astype(F32).astype(BF16)
-    acc_s[...] = dot(t_ref[...], w_ref[half:, :])
     scale = 1.0 / jnp.sqrt(F32(HD))
+    total = 12 * NB
+    for c in copies[:4] + copies[5:8]:
+        c.wait()
     first = nb_ref[0, 0]
-    total = 12 * NB
-    for c in copies[:4]:
-        c.wait()
-    for j in range(NB):
-        rows = slice(j * BLK, (j + 1) * BLK)
+    copies[8].start()
+
+    def select(j):
         starts = []
         lane = lax.broadcasted_iota(jnp.int32, (BLK, MAXNB * BLK), 1)
         keep = lane < cnt_ref[j] * BLK
@@ -167,24 +186,34 @@
         def listed(lo):
             return jnp.concatenate([win[pl.ds(at, BLK), lo : lo + HD] for at in starts], axis=0)
 
-        heads = range(SHEADS)
-        cols = [slice(h * HD, (h + 1) * HD) for h in heads]
-        ss = [jnp.where(keep, dot_t(q_ref[rows, cols[h]], listed(h * HD)) * scale, NEG) for h in heads]
-        tops = [jnp.max(s, axis=-1, keepdims=True) for s in ss]
-        es = [jnp.exp(s - top) for s, top in zip(ss, tops)]
+        return slice(j * BLK, (j + 1) * BLK), keep, listed
+
+    def score(item):
+        (rows, keep, listed), h = item
+        return jnp.where(keep, dot_t(q_ref[rows, h * HD : (h + 1) * HD], listed(h * HD)), NEG)
+
+    items = [(sel, h) for sel in map(select, range(NB)) for h in range(SHEADS)]
+    step = 2
+    now = [score(item) for item in items[:step]]
+    for g in range(0, len(items), step):
+        ahead = [score(item) for item in items[g + step : g + 2 * step]]
+        tops = [jnp.max(s, axis=-1, keepdims=True) for s in now]
+        es = [jnp.exp2((s - top) * (scale * LOG2E)) for s, top in zip(now, tops)]
         invs = [1.0 / jnp.sum(e, axis=-1, keepdims=True) for e in es]
-        ps = [(e * inv).astype(BF16) for e, inv in zip(es, invs)]
-        for h in heads:
-            blk_s[rows, cols[h]] = dot(ps[h], listed(half + h * HD)).astype(BF16)
-    copies[4].wait()
+        for ((rows, _, listed), h), e, inv in zip(items[g : g + step], es, invs):
+            o = dot(e.astype(BF16), listed(half + h * HD)) * inv
+            blk_s[rows, h * HD : (h + 1) * HD] = o.astype(BF16)
+        now = ahead
+    copies[8].wait()
     gate = cond_ref[2:3, :]
     outs = []
-    for j in range(NB):
-        rows = slice(j * BLK, (j + 1) * BLK)
-        sp = dot(unperm[rows, :], blk_s[...]).astype(BF16)
-        mixed = dot(sp, w_ref[:half, :]) + acc_s[rows, :]
-        o_s[rows, :] = (x_s[rows, :].astype(F32) + gate * mixed).astype(BF16)
-        out = pltpu.make_async_copy(o_s.at[rows], o_hbm.at[0, rows], sem.at[5 + j])
+    sp = dot(unperm, blk_s[...]).astype(BF16)
+    quarter = width // 4
+    for i in range(4):
+        cs = slice(i * quarter, (i + 1) * quarter)
+        mixed = dot(sp, w_ref[:half, cs]) + acc_s[:, cs]
+        o_s[:, cs] = (x_s[:, cs].astype(F32) + gate[:, cs] * mixed).astype(BF16)
+        out = pltpu.make_async_copy(o_s.at[:, cs], o_hbm.at[0, :, cs], sem.at[9 + i])
         out.start()
         outs.append(out)
     for out in outs:
@@ -193,7 +222,6 @@
 
 HB = pl.BlockSpec(memory_space=pltpu.HBM)
 VM = pl.BlockSpec(memory_space=pltpu.VMEM)
-SM = pl.BlockSpec(memory_space=pltpu.SMEM)
 DMA = pltpu.SemaphoreType.DMA
 
 
@@ -222,10 +250,18 @@
     seen = lax.all_to_all(latent.reshape(CLIP, per, width), "member", 0, 0, tiled=True)
     kv, mod = call(
         spatial_keyval,
-        [HB, VM, VM, HB],
+        [HB, HB, HB, HB],
         (HB, HB),
         (arr((tokens, width), BF16), arr((tokens, width), BF16)),
-        [room(tokens, width), room(width, width), room(tokens, width), room(tokens, width), DMA((6,))],
+        [
+            pltpu.VMEM((3, width), F32),
+            pltpu.VMEM((1, tokens), jnp.int32),
+            room(tokens, width),
+            room(width, width),
+            room(tokens, width),
+            room(tokens, width),
+            DMA((10,)),
+        ],
     )(latent, cond, slot_row, w_qkv)
     count = lax.axis_size("space")
     left = lax.ppermute(kv, "space", [(i, (i + 1) % count) for i in range(count)])
@@ -239,31 +275,36 @@
     )(mod, w_qkv)
     t_out = call(
         temporal,
-        [VM, VM, HB],
+        [VM, HB, HB],
         HB,
         arr((CLIP, per, half), BF16),
         [
+            pltpu.VMEM((3, width), F32),
             room(width, 3 * half),
             room(tokens, width),
             room(CLIP, per, 3 * half),
             room(CLIP, per, half),
-            DMA((3 + per // (128 // CLIP),)),
+            DMA((8,)),
         ],
     )(near(seen), cond, w_qkv)
     back = lax.all_to_all(t_out, "member", 0, 0, tiled=True).reshape(tokens, half)
     return call(
         finish,
-        [SM, SM, HB, VM, VM, HB, HB, HB, HB, VM, VM],
+        [HB] * 9 + [VM, VM],
         HB,
         arr((1, tokens, width), BF16),
         [
+            pltpu.SMEM((NB, MAXNB), jnp.int32),
+            pltpu.SMEM((NB,), jnp.int32),
+            pltpu.VMEM((3, width), F32),
+            pltpu.VMEM((1, tokens), jnp.int32),
             room(tokens, width),
             room(tokens, half),
             room(3 * tokens, width),
             room(tokens, half),
             pltpu.VMEM((tokens, width), F32),
             room(tokens, width),
-            DMA((9,)),
+            DMA((13,)),
         ],
     )(neighbours, counts, latent, cond, slot_row, q, kv, left, right, near(back), near(w_out))
 

time: 56.4 us -> 55.1 us (0.977)
  the two profiles are of different devices: /device:TPU:18 before, /device:TPU:2 now
where the time goes in v3:
time: 55.1 us; the launch traced here: 54.7 us
  starting transfers between devices  25.2 us (46%)
  Pallas kernels  20.8 us (38%)
  waiting for transfers between devices  8.61 us (16%)
    all_to_all x1, starting transfers between devices, body(): lax.all_to_all(latent.reshape(CLIP, per, width), 'member', 0, 0, tiled=True)  13 us
    pallas_call x1, Pallas kernels, body(): call(finish, [HB] * 9 + [VM, VM], HB, arr((1, tokens, width), BF16), [plt...  6.92 us
    ppermute x1, waiting for transfers between devices, body(): lax.ppermute(kv, 'space', [((i + 1) % count, i) for i in range(count)])  6.2 us
    pallas_call x1, Pallas kernels, body(): call(temporal, [VM, HB, HB], HB, arr((CLIP, per, half), BF16), [pltpu.VME...  5.97 us
    all_to_all x1, starting transfers between devices, body(): lax.all_to_all(t_out, 'member', 0, 0, tiled=True).reshape(tokens, half)  5.84 us
    pallas_call x1, Pallas kernels, body(): call(spatial_keyval, [HB, HB, HB, HB], (HB, HB), (arr((tokens, width), BF...  4.84 us
    ppermute x1, starting transfers between devices, body(): lax.ppermute(kv, 'space', [((i + 1) % count, i) for i in range(count)])  4.47 us
    pallas_call x1, Pallas kernels, body(): call(spatial_query, [HB, HB], VM, arr((tokens, half), BF16), [room(tokens...  3.06 us
  transfers between devices with their start and end apart: 4, of which 2 were waited for; matrix products, arithmetic and copies ran while one was open for 0% of the time, Pallas kernels for 25%

profile of v3, /device:TPU:2, one launch (start us, length us, event | category | flops | bytes accessed | tf_op | source)
XLA Modules:
  0.0 54.7 jit_solution(9458645658971811306)
XLA Ops:
  0.0 13.0 %all-to-all-start = ((bf16[8,64,1024]{2,1,0:T(8,128)(2,1)}), bf16[8,64,1024]{2,1,0:T(8,128)(2,1)S(1)}, u32[]{:S(2)}, u32[]{:S(2)}) async-start(bf16[8,64,1024]{2,1,0:T(8,128)(2,1)} %bitcast.4), calls=%async_computation | async-start | bytes 2097152 | tf_op jit(solution)/shard_map/all_to_all | solution.py:250
  13.0 4.8 %spatial_keyval.1 = (bf16[512,1024]{1,0:T(8,128)(2,1)}, bf16[512,1024]{1,0:T(8,128)(2,1)}) custom-call(bf16[1,512,1024]{2,1,0:T(8,128)(2,1)} %x_hbm.3, f32[3,1024]{1,0:T(4,128)} %cond_hbm.5, s32[1,512]{1,0:T(1,128)} %bitcast.5, bf16[1024,3072]{1,0:T(8,128)(2,1)} %w_hbm.5), custom_call_target="tpu_custom_call" | custom-call | tf_op jit(solution)/shard_map/spatial_keyval/pallas_call | solution.py:251
  17.8 4.5 %collective-permute-start.1 = (bf16[512,1024]{1,0:T(8,128)(2,1)}, bf16[512,1024]{1,0:T(8,128)(2,1)}, u32[]{:S(2)}, u32[]{:S(2)}) collective-permute-start(bf16[512,1024]{1,0:T(8,128)(2,1)} %get-tuple-element.8.kv_hbm), channel_id=1, source_target_pairs={{64,0},{128,64},{192,128},{256,192},{320,256},{384,320},{448,384},... | collective-permute-start | bytes 3145736 | tf_op jit(solution)/shard_map/ppermute | solution.py:268
  22.3 1.9 %collective-permute-start = (bf16[512,1024]{1,0:T(8,128)(2,1)}, bf16[512,1024]{1,0:T(8,128)(2,1)}, u32[]{:S(2)}, u32[]{:S(2)}) collective-permute-start(bf16[512,1024]{1,0:T(8,128)(2,1)} %get-tuple-element.8.kv_hbm), channel_id=1, source_target_pairs={{0,64},{64,128},{128,192},{192,256},{256,320},{320,384},{384,448},... | collective-permute-start | bytes 3145736 | tf_op jit(solution)/shard_map/ppermute | solution.py:267
  24.2 0.0 all-to-all-done.x_ref
  24.2 6.0 %temporal.1 = bf16[8,64,512]{2,1,0:T(8,128)(2,1)} custom-call(bf16[8,64,1024]{2,1,0:T(8,128)(2,1)S(1)} %all-to-all-done.x_ref, f32[3,1024]{1,0:T(4,128)} %cond_hbm.5, bf16[1024,3072]{1,0:T(8,128)(2,1)} %w_hbm.5), custom_call_target="tpu_custom_call" | custom-call | tf_op jit(solution)/shard_map/temporal/pallas_call | solution.py:276
  30.2 0.0 copy-start
  30.2 5.8 %all-to-all-start.1 = ((bf16[8,64,512]{2,1,0:T(8,128)(2,1)}), bf16[8,64,512]{2,1,0:T(8,128)(2,1)S(1)}, u32[]{:S(2)}, u32[]{:S(2)}) async-start(bf16[8,64,512]{2,1,0:T(8,128)(2,1)} %temporal.1), calls=%async_computation.1 | async-start | bytes 1048576 | tf_op jit(solution)/shard_map/all_to_all | solution.py:290
  36.1 3.1 %spatial_query.1.q_hbm = bf16[512,512]{1,0:T(8,128)(2,1)} custom-call(bf16[512,1024]{1,0:T(8,128)(2,1)} %get-tuple-element.7.mod_hbm, bf16[1024,3072]{1,0:T(8,128)(2,1)} %w_hbm.5), custom_call_target="tpu_custom_call" | custom-call | tf_op jit(solution)/shard_map/spatial_query/pallas_call | solution.py:269
  39.1 6.2 %collective-permute-done.1.right_hbm = bf16[512,1024]{1,0:T(8,128)(2,1)} collective-permute-done((bf16[512,1024]{1,0:T(8,128)(2,1)}, bf16[512,1024]{1,0:T(8,128)(2,1)}, u32[]{:S(2)}, u32[]{:S(2)}) %collective-permute-start.1) | collective-permute-done | bytes 1048608 | tf_op jit(solution)/shard_map/ppermute | solution.py:268
  45.3 2.4 %collective-permute-done.left_hbm = bf16[512,1024]{1,0:T(8,128)(2,1)} collective-permute-done((bf16[512,1024]{1,0:T(8,128)(2,1)}, bf16[512,1024]{1,0:T(8,128)(2,1)}, u32[]{:S(2)}, u32[]{:S(2)}) %collective-permute-start) | collective-permute-done | bytes 1048608 | tf_op jit(solution)/shard_map/ppermute | solution.py:267
  47.7 0.0 all-to-all-done.1
  47.7 0.0 copy-done
  47.7 6.9 %finish.1 = bf16[1,512,1024]{2,1,0:T(8,128)(2,1)} custom-call(s32[4,4]{1,0:T(4,128)} %nb_hbm.1, s32[4]{0:T(128)} %cnt_hbm.1, bf16[1,512,1024]{2,1,0:T(8,128)(2,1)} %x_hbm.3, f32[3,1024]{1,0:T(4,128)} %cond_hbm.5, s32[1,512]{1,0:T(1,128)} %bitcast.6, bf16[512,512]{1,0:T(8,128)(2,1)} %spatial_query.1.q_hbm, bf16[512,1024]{1,0:T(8,128)(2,1)} %get-tuple-element.8.kv_hbm, ...), custom_call_target="tpu_custom_call" | custom-call | tf_op jit(solution)/shard_map/finish/pallas_call | solution.py:291
Async XLA Ops:
  0.0 24.2 %all-to-all-start = ((bf16[8,64,1024]{2,1,0:T(8,128)(2,1)}), bf16[8,64,1024]{2,1,0:T(8,128)(2,1)S(1)}, u32[]{:S(2)}, u32[]{:S(2)}) async-start(bf16[8,64,1024]{2,1,0:T(8,128)(2,1)} %bitcast.4), calls=%async_computation | async-start | bytes 2097152 | tf_op jit(solution)/shard_map/all_to_all | solution.py:250
  17.8 27.5 %collective-permute-start.1 = (bf16[512,1024]{1,0:T(8,128)(2,1)}, bf16[512,1024]{1,0:T(8,128)(2,1)}, u32[]{:S(2)}, u32[]{:S(2)}) collective-permute-start(bf16[512,1024]{1,0:T(8,128)(2,1)} %get-tuple-element.8.kv_hbm), channel_id=1, source_target_pairs={{64,0},{128,64},{192,128},{256,192},{320,256},{384,320},{448,384},... | collective-permute-start | bytes 3145736 | tf_op jit(solution)/shard_map/ppermute | solution.py:268
  22.3 25.4 %collective-permute-start = (bf16[512,1024]{1,0:T(8,128)(2,1)}, bf16[512,1024]{1,0:T(8,128)(2,1)}, u32[]{:S(2)}, u32[]{:S(2)}) collective-permute-start(bf16[512,1024]{1,0:T(8,128)(2,1)} %get-tuple-element.8.kv_hbm), channel_id=1, source_target_pairs={{0,64},{64,128},{128,192},{192,256},{256,320},{320,384},{384,448},... | collective-permute-start | bytes 3145736 | tf_op jit(solution)/shard_map/ppermute | solution.py:267
  30.2 17.5 %copy-start = (bf16[1024,1024]{1,0:T(8,128)(2,1)S(1)}, bf16[1024,1024]{1,0:T(8,128)(2,1)}, u32[]{:S(2)}) copy-start(bf16[1024,1024]{1,0:T(8,128)(2,1)} %w_ref.1) | copy-start | bytes 6291460
  30.2 17.5 %all-to-all-start.1 = ((bf16[8,64,512]{2,1,0:T(8,128)(2,1)}), bf16[8,64,512]{2,1,0:T(8,128)(2,1)S(1)}, u32[]{:S(2)}, u32[]{:S(2)}) async-start(bf16[8,64,512]{2,1,0:T(8,128)(2,1)} %temporal.1), calls=%async_computation.1 | async-start | bytes 1048576 | tf_op jit(solution)/shard_map/all_to_all | solution.py:290

commit v4 on v3

--- a/solution.py
+++ b/solution.py
@@ -145,34 +145,50 @@
         out.wait()
 
 
-def finish(nb_hbm, cnt_hbm, x_hbm, cond_hbm, slot_hbm, q_hbm, kv_hbm, left_hbm, right_hbm, t_ref, w_ref, o_hbm,
-           nb_ref, cnt_ref, cond_ref, slot_ref, x_s, q_ref, win, blk_s, acc_s, o_s, sem):
-    tokens, width = x_s.shape
+def temporal_out(t_ref, w_hbm, x_hbm, cond_hbm, o_ref, w_s, x_s, cond_ref, sem):
+    half = t_ref.shape[1]
+    copies = [
+        (w_hbm.at[pl.ds(half, half)], w_s),
+        (x_hbm.at[0], x_s),
+        (cond_hbm, cond_ref),
+    ]
+    copies = [pltpu.make_async_copy(a, b, sem.at[i]) for i, (a, b) in enumerate(copies)]
+    for c in copies:
+        c.start()
+    for c in copies:
+        c.wait()
+    o_ref[...] = x_s[...].astype(F32) + cond_ref[2:3, :] * dot(t_ref[...], w_s[...])
+
+
+def finish(nb_hbm, cnt_hbm, acc_hbm, cond_hbm, slot_hbm, q_hbm, kv_hbm, left_ref, right_ref, w_hbm, o_hbm,
+           nb_ref, cnt_ref, cond_ref, slot_ref, q_ref, win, blk_s, acc_s, w_s, o_s, sem):
+    tokens, width = acc_s.shape
     half = width // 2
     copies = [
-        (left_hbm, win.at[pl.ds(0, tokens)]),
-        (right_hbm, win.at[pl.ds(2 * tokens, tokens)]),
-        (kv_hbm, win.at[pl.ds(tokens, tokens)]),
-        (q_hbm, q_ref),
         (slot_hbm, slot_ref),
         (nb_hbm, nb_ref),
         (cnt_hbm, cnt_ref),
+        (q_hbm, q_ref),
+        (kv_hbm, win.at[pl.ds(tokens, tokens)]),
         (cond_hbm, cond_ref),
-        (x_hbm.at[0], x_s),
+        (w_hbm.at[pl.ds(0, half)], w_s),
+        (acc_hbm, acc_s),
     ]
     copies = [pltpu.make_async_copy(a, b, sem.at[i]) for i, (a, b) in enumerate(copies)]
-    for c in copies[4:8] + copies[:4]:
+    for c in copies[:6]:
         c.start()
-    acc_s[...] = dot(t_ref[...], w_ref[half:, :])
-    copies[4].wait()
+    win[:tokens, :] = left_ref[...]
+    win[2 * tokens :, :] = right_ref[...]
+    copies[0].wait()
     tok = lax.broadcasted_iota(jnp.int32, (tokens, tokens), 0)
     unperm = (tok == slot_ref[...]).astype(F32).astype(BF16)
     scale = 1.0 / jnp.sqrt(F32(HD))
     total = 12 * NB
-    for c in copies[:4] + copies[5:8]:
+    for c in copies[1:6]:
         c.wait()
+    for c in copies[6:]:
+        c.start()
     first = nb_ref[0, 0]
-    copies[8].start()
 
     def select(j):
         starts = []
@@ -204,16 +220,16 @@
             o = dot(e.astype(BF16), listed(half + h * HD)) * inv
             blk_s[rows, h * HD : (h + 1) * HD] = o.astype(BF16)
         now = ahead
-    copies[8].wait()
+    copies[6].wait()
+    copies[7].wait()
     gate = cond_ref[2:3, :]
     outs = []
     sp = dot(unperm, blk_s[...]).astype(BF16)
     quarter = width // 4
     for i in range(4):
         cs = slice(i * quarter, (i + 1) * quarter)
-        mixed = dot(sp, w_ref[:half, cs]) + acc_s[:, cs]
-        o_s[:, cs] = (x_s[:, cs].astype(F32) + gate[:, cs] * mixed).astype(BF16)
-        out = pltpu.make_async_copy(o_s.at[:, cs], o_hbm.at[0, :, cs], sem.at[9 + i])
+        o_s[:, cs] = (acc_s[:, cs] + gate[:, cs] * dot(sp, w_s[:, cs])).astype(BF16)
+        out = pltpu.make_async_copy(o_s.at[:, cs], o_hbm.at[0, :, cs], sem.at[8 + i])
         out.start()
         outs.append(out)
     for out in outs:
@@ -288,9 +304,16 @@
         ],
     )(near(seen), cond, w_qkv)
     back = lax.all_to_all(t_out, "member", 0, 0, tiled=True).reshape(tokens, half)
+    acc = call(
+        temporal_out,
+        [VM, HB, HB, HB],
+        VM,
+        arr((tokens, width), F32),
+        [room(half, width), room(tokens, width), pltpu.VMEM((3, width), F32), DMA((3,))],
+    )(near(back), w_out, latent, cond)
     return call(
         finish,
-        [HB] * 9 + [VM, VM],
+        [HB] * 7 + [VM, VM, HB],
         HB,
         arr((1, tokens, width), BF16),
         [
@@ -298,15 +321,15 @@
             pltpu.SMEM((NB,), jnp.int32),
             pltpu.VMEM((3, width), F32),
             pltpu.VMEM((1, tokens), jnp.int32),
-            room(tokens, width),
             room(tokens, half),
             room(3 * tokens, width),
             room(tokens, half),
             pltpu.VMEM((tokens, width), F32),
-            room(tokens, width),
-            DMA((13,)),
+            room(half, width),
+            room(tokens, width),
+            DMA((12,)),
         ],
-    )(neighbours, counts, latent, cond, slot_row, q, kv, left, right, near(back), near(w_out))
+    )(neighbours, counts, acc, cond, slot_row, q, kv, near(left), near(right), w_out)
 
 
 def solution(mesh):

time: 55.1 us -> 56 us (1.016)
  the two profiles are of different devices: /device:TPU:2 before, /device:TPU:18 now
where the time goes in v4:
time: 56 us; the launch traced here: 55.5 us
  Pallas kernels  25.4 us (45%)
  starting transfers between devices  25.1 us (45%)
  waiting for transfers between devices  5.04 us (9%)
    ppermute x1, starting transfers between devices, body(): lax.ppermute(kv, 'space', [((i + 1) % count, i) for i in range(count)])  11.6 us
    pallas_call x1, Pallas kernels, body(): call(finish, [HB] * 7 + [VM, VM, HB], HB, arr((1, tokens, width), BF16),...  7.77 us
    pallas_call x1, Pallas kernels, body(): call(temporal, [VM, HB, HB], HB, arr((CLIP, per, half), BF16), [pltpu.VME...  6 us
    all_to_all x1, starting transfers between devices, body(): lax.all_to_all(latent.reshape(CLIP, per, width), 'member', 0, 0, tiled=True)  5.84 us
    all_to_all x1, starting transfers between devices, body(): lax.all_to_all(t_out, 'member', 0, 0, tiled=True).reshape(tokens, half)  5.71 us
    pallas_call x1, Pallas kernels, body(): call(spatial_keyval, [HB, HB, HB, HB], (HB, HB), (arr((tokens, width), BF...  4.88 us
    pallas_call x1, Pallas kernels, body(): call(temporal_out, [VM, HB, HB, HB], VM, arr((tokens, width), F32), [room...  3.64 us
    all_to_all x1, waiting for transfers between devices, body(): lax.all_to_all(t_out, 'member', 0, 0, tiled=True).reshape(tokens, half)  3.54 us
  transfers between devices with their start and end apart: 4, of which 2 were waited for; matrix products, arithmetic and copies ran while one was open for 0% of the time, Pallas kernels for 32%

profile of v4, /device:TPU:18, one launch (start us, length us, event | category | flops | bytes accessed | tf_op | source)
XLA Modules:
  0.0 55.5 jit_solution(16996273741890874219)
XLA Ops:
  0.0 5.8 %all-to-all-start = ((bf16[8,64,1024]{2,1,0:T(8,128)(2,1)}), bf16[8,64,1024]{2,1,0:T(8,128)(2,1)S(1)}, u32[]{:S(2)}, u32[]{:S(2)}) async-start(bf16[8,64,1024]{2,1,0:T(8,128)(2,1)} %bitcast.4), calls=%async_computation | async-start | bytes 2097152 | tf_op jit(solution)/shard_map/all_to_all | solution.py:266
  5.8 4.9 %spatial_keyval.1 = (bf16[512,1024]{1,0:T(8,128)(2,1)}, bf16[512,1024]{1,0:T(8,128)(2,1)}) custom-call(bf16[1,512,1024]{2,1,0:T(8,128)(2,1)} %x_hbm.3, f32[3,1024]{1,0:T(4,128)} %cond_hbm.7, s32[1,512]{1,0:T(1,128)} %bitcast.5, bf16[1024,3072]{1,0:T(8,128)(2,1)} %w_hbm.8), custom_call_target="tpu_custom_call" | custom-call | tf_op jit(solution)/shard_map/spatial_keyval/pallas_call | solution.py:267
  10.7 11.6 %collective-permute-start.1 = (bf16[512,1024]{1,0:T(8,128)(2,1)}, bf16[512,1024]{1,0:T(8,128)(2,1)S(1)}, u32[]{:S(2)}, u32[]{:S(2)}) collective-permute-start(bf16[512,1024]{1,0:T(8,128)(2,1)} %get-tuple-element.8.kv_hbm), channel_id=1, source_target_pairs={{64,0},{128,64},{192,128},{256,192},{320,256},{384,320},{448,384},... | collective-permute-start | bytes 3145736 | tf_op jit(solution)/shard_map/ppermute | solution.py:284
  22.3 1.9 %collective-permute-start = (bf16[512,1024]{1,0:T(8,128)(2,1)}, bf16[512,1024]{1,0:T(8,128)(2,1)}, u32[]{:S(2)}, u32[]{:S(2)}) collective-permute-start(bf16[512,1024]{1,0:T(8,128)(2,1)} %get-tuple-element.8.kv_hbm), channel_id=1, source_target_pairs={{0,64},{64,128},{128,192},{192,256},{256,320},{320,384},{384,448},... | collective-permute-start | bytes 3145736 | tf_op jit(solution)/shard_map/ppermute | solution.py:283
  24.3 0.0 all-to-all-done.x_ref
  24.3 6.0 %temporal.1 = bf16[8,64,512]{2,1,0:T(8,128)(2,1)} custom-call(bf16[8,64,1024]{2,1,0:T(8,128)(2,1)S(1)} %all-to-all-done.x_ref, f32[3,1024]{1,0:T(4,128)} %cond_hbm.7, bf16[1024,3072]{1,0:T(8,128)(2,1)} %w_hbm.8), custom_call_target="tpu_custom_call" | custom-call | tf_op jit(solution)/shard_map/temporal/pallas_call | solution.py:292
  30.3 5.7 %all-to-all-start.1 = ((bf16[8,64,512]{2,1,0:T(8,128)(2,1)}), bf16[8,64,512]{2,1,0:T(8,128)(2,1)S(1)}, u32[]{:S(2)}, u32[]{:S(2)}) async-start(bf16[8,64,512]{2,1,0:T(8,128)(2,1)} %temporal.1), calls=%async_computation.1 | async-start | bytes 1048576 | tf_op jit(solution)/shard_map/all_to_all | solution.py:306
  36.0 3.1 %spatial_query.1.q_hbm = bf16[512,512]{1,0:T(8,128)(2,1)} custom-call(bf16[512,1024]{1,0:T(8,128)(2,1)} %get-tuple-element.7.mod_hbm, bf16[1024,3072]{1,0:T(8,128)(2,1)} %w_hbm.8), custom_call_target="tpu_custom_call" | custom-call | tf_op jit(solution)/shard_map/spatial_query/pallas_call | solution.py:285
  39.1 3.5 %all-to-all-done.1 = bf16[8,64,512]{2,1,0:T(8,128)(2,1)S(1)} async-done(((bf16[8,64,512]{2,1,0:T(8,128)(2,1)}), bf16[8,64,512]{2,1,0:T(8,128)(2,1)S(1)}, u32[]{:S(2)}, u32[]{:S(2)}) %all-to-all-start.1) | async-done | bytes 524320 | tf_op jit(solution)/shard_map/all_to_all | solution.py:306
  42.6 3.6 %temporal_out.1.acc_hbm = f32[512,1024]{1,0:T(8,128)} custom-call(bf16[512,512]{1,0:T(8,128)(2,1)S(1)} %bitcast.3, bf16[1024,1024]{1,0:T(8,128)(2,1)} %w_hbm.9, bf16[1,512,1024]{2,1,0:T(8,128)(2,1)} %x_hbm.3, f32[3,1024]{1,0:T(4,128)} %cond_hbm.7), custom_call_target="tpu_custom_call" | custom-call | tf_op jit(solution)/shard_map/temporal_out/pallas_call | solution.py:307
  46.3 0.0 collective-permute-done.1.right_ref
  46.3 1.5 %collective-permute-done.left_ref = bf16[512,1024]{1,0:T(8,128)(2,1)} collective-permute-done((bf16[512,1024]{1,0:T(8,128)(2,1)}, bf16[512,1024]{1,0:T(8,128)(2,1)}, u32[]{:S(2)}, u32[]{:S(2)}) %collective-permute-start) | collective-permute-done | bytes 1048608 | tf_op jit(solution)/shard_map/ppermute | solution.py:283
  47.8 7.8 %finish.1 = bf16[1,512,1024]{2,1,0:T(8,128)(2,1)} custom-call(s32[4,4]{1,0:T(4,128)} %nb_hbm.1, s32[4]{0:T(128)} %cnt_hbm.1, f32[512,1024]{1,0:T(8,128)} %temporal_out.1.acc_hbm, f32[3,1024]{1,0:T(4,128)} %cond_hbm.7, s32[1,512]{1,0:T(1,128)} %bitcast.6, bf16[512,512]{1,0:T(8,128)(2,1)} %spatial_query.1.q_hbm, bf16[512,1024]{1,0:T(8,128)(2,1)} %get-tuple-element.8.kv_hbm, ...), custom_call_target="tpu_custom_call" | custom-call | tf_op jit(solution)/shard_map/finish/pallas_call | solution.py:314
Async XLA Ops:
  0.0 24.3 %all-to-all-start = ((bf16[8,64,1024]{2,1,0:T(8,128)(2,1)}), bf16[8,64,1024]{2,1,0:T(8,128)(2,1)S(1)}, u32[]{:S(2)}, u32[]{:S(2)}) async-start(bf16[8,64,1024]{2,1,0:T(8,128)(2,1)} %bitcast.4), calls=%async_computation | async-start | bytes 2097152 | tf_op jit(solution)/shard_map/all_to_all | solution.py:266
  10.7 35.5 %collective-permute-start.1 = (bf16[512,1024]{1,0:T(8,128)(2,1)}, bf16[512,1024]{1,0:T(8,128)(2,1)S(1)}, u32[]{:S(2)}, u32[]{:S(2)}) collective-permute-start(bf16[512,1024]{1,0:T(8,128)(2,1)} %get-tuple-element.8.kv_hbm), channel_id=1, source_target_pairs={{64,0},{128,64},{192,128},{256,192},{320,256},{384,320},{448,384},... | collective-permute-start | bytes 3145736 | tf_op jit(solution)/shard_map/ppermute | solution.py:284
  22.3 25.4 %collective-permute-start = (bf16[512,1024]{1,0:T(8,128)(2,1)}, bf16[512,1024]{1,0:T(8,128)(2,1)}, u32[]{:S(2)}, u32[]{:S(2)}) collective-permute-start(bf16[512,1024]{1,0:T(8,128)(2,1)} %get-tuple-element.8.kv_hbm), channel_id=1, source_target_pairs={{0,64},{64,128},{128,192},{192,256},{256,320},{320,384},{384,448},... | collective-permute-start | bytes 3145736 | tf_op jit(solution)/shard_map/ppermute | solution.py:283
  30.3 12.3 %all-to-all-start.1 = ((bf16[8,64,512]{2,1,0:T(8,128)(2,1)}), bf16[8,64,512]{2,1,0:T(8,128)(2,1)S(1)}, u32[]{:S(2)}, u32[]{:S(2)}) async-start(bf16[8,64,512]{2,1,0:T(8,128)(2,1)} %temporal.1), calls=%async_computation.1 | async-start | bytes 1048576 | tf_op jit(solution)/shard_map/all_to_all | solution.py:306

commit v5 on v4

--- a/solution.py
+++ b/solution.py
@@ -145,9 +145,10 @@
         out.wait()
 
 
-def temporal_out(t_ref, w_hbm, x_hbm, cond_hbm, o_ref, w_s, x_s, cond_ref, sem):
-    half = t_ref.shape[1]
+def temporal_out(t_hbm, w_hbm, x_hbm, cond_hbm, o_ref, t_s, w_s, x_s, cond_ref, sem):
+    tokens, half = t_s.shape
     copies = [
+        (t_hbm, t_s),
         (w_hbm.at[pl.ds(half, half)], w_s),
         (x_hbm.at[0], x_s),
         (cond_hbm, cond_ref),
@@ -157,7 +158,7 @@
         c.start()
     for c in copies:
         c.wait()
-    o_ref[...] = x_s[...].astype(F32) + cond_ref[2:3, :] * dot(t_ref[...], w_s[...])
+    o_ref[...] = x_s[...].astype(F32) + cond_ref[2:3, :] * dot(t_s[...], w_s[...])
 
 
 def finish(nb_hbm, cnt_hbm, acc_hbm, cond_hbm, slot_hbm, q_hbm, kv_hbm, left_ref, right_ref, w_hbm, o_hbm,
@@ -306,11 +307,11 @@
     back = lax.all_to_all(t_out, "member", 0, 0, tiled=True).reshape(tokens, half)
     acc = call(
         temporal_out,
-        [VM, HB, HB, HB],
+        [HB, HB, HB, HB],
         VM,
         arr((tokens, width), F32),
-        [room(half, width), room(tokens, width), pltpu.VMEM((3, width), F32), DMA((3,))],
-    )(near(back), w_out, latent, cond)
+        [room(tokens, half), room(half, width), room(tokens, width), pltpu.VMEM((3, width), F32), DMA((4,))],
+    )(back, w_out, latent, cond)
     return call(
         finish,
         [HB] * 7 + [VM, VM, HB],

time: 56 us -> 55.3 us (0.987)
  the two profiles are of different devices: /device:TPU:18 before, /device:TPU:16 now
where the time goes in v5:
time: 55.3 us; the launch traced here: 54.9 us
  starting transfers between devices  24.5 us (44%)
  Pallas kernels  24.3 us (44%)
  waiting for transfers between devices  5.22 us (9%)
  local copies, waits for them, and re-layouts  0.79 us (1%)
    ppermute x1, starting transfers between devices, body(): lax.ppermute(kv, 'space', [((i + 1) % count, i) for i in range(count)])  11.9 us
    pallas_call x1, Pallas kernels, body(): call(finish, [HB] * 7 + [VM, VM, HB], HB, arr((1, tokens, width), BF16),...  6.54 us
    pallas_call x1, Pallas kernels, body(): call(temporal, [VM, HB, HB], HB, arr((CLIP, per, half), BF16), [pltpu.VME...  5.97 us
    all_to_all x1, starting transfers between devices, body(): lax.all_to_all(t_out, 'member', 0, 0, tiled=True).reshape(tokens, half)  5.43 us
    all_to_all x1, starting transfers between devices, body(): lax.all_to_all(latent.reshape(CLIP, per, width), 'member', 0, 0, tiled=True)  5.31 us
    all_to_all x1, waiting for transfers between devices, body(): lax.all_to_all(t_out, 'member', 0, 0, tiled=True).reshape(tokens, half)  5.21 us
    pallas_call x1, Pallas kernels, body(): call(spatial_keyval, [HB, HB, HB, HB], (HB, HB), (arr((tokens, width), BF...  4.89 us
    pallas_call x1, Pallas kernels, body(): call(temporal_out, [HB, HB, HB, HB], VM, arr((tokens, width), F32), [room...  3.8 us
  transfers between devices with their start and end apart: 4, of which 1 were waited for; matrix products, arithmetic and copies ran while one was open for 0% of the time, Pallas kernels for 32%

profile of v5, /device:TPU:16, one launch (start us, length us, event | category | flops | bytes accessed | tf_op | source)
XLA Modules:
  0.0 54.9 jit_solution(11615703894176213513)
XLA Ops:
  0.0 5.3 %all-to-all-start = ((bf16[8,64,1024]{2,1,0:T(8,128)(2,1)}), bf16[8,64,1024]{2,1,0:T(8,128)(2,1)S(1)}, u32[]{:S(2)}, u32[]{:S(2)}) async-start(bf16[8,64,1024]{2,1,0:T(8,128)(2,1)} %bitcast.3), calls=%async_computation | async-start | bytes 2097152 | tf_op jit(solution)/shard_map/all_to_all | solution.py:267
  5.3 4.9 %spatial_keyval.1 = (bf16[512,1024]{1,0:T(8,128)(2,1)}, bf16[512,1024]{1,0:T(8,128)(2,1)}) custom-call(bf16[1,512,1024]{2,1,0:T(8,128)(2,1)} %x_hbm.3, f32[3,1024]{1,0:T(4,128)} %cond_hbm.7, s32[1,512]{1,0:T(1,128)} %bitcast.5, bf16[1024,3072]{1,0:T(8,128)(2,1)} %w_hbm.8), custom_call_target="tpu_custom_call" | custom-call | tf_op jit(solution)/shard_map/spatial_keyval/pallas_call | solution.py:268
  10.2 11.9 %collective-permute-start.1 = (bf16[512,1024]{1,0:T(8,128)(2,1)}, bf16[512,1024]{1,0:T(8,128)(2,1)S(1)}, u32[]{:S(2)}, u32[]{:S(2)}) collective-permute-start(bf16[512,1024]{1,0:T(8,128)(2,1)} %get-tuple-element.8.kv_hbm), channel_id=1, source_target_pairs={{64,0},{128,64},{192,128},{256,192},{320,256},{384,320},{448,384},... | collective-permute-start | bytes 3145736 | tf_op jit(solution)/shard_map/ppermute | solution.py:285
  22.1 1.9 %collective-permute-start = (bf16[512,1024]{1,0:T(8,128)(2,1)}, bf16[512,1024]{1,0:T(8,128)(2,1)S(1)}, u32[]{:S(2)}, u32[]{:S(2)}) collective-permute-start(bf16[512,1024]{1,0:T(8,128)(2,1)} %get-tuple-element.8.kv_hbm), channel_id=1, source_target_pairs={{0,64},{64,128},{128,192},{192,256},{256,320},{320,384},{384,448},... | collective-permute-start | bytes 3145736 | tf_op jit(solution)/shard_map/ppermute | solution.py:284
  24.0 0.0 all-to-all-done.x_ref
  24.0 6.0 %temporal.1 = bf16[8,64,512]{2,1,0:T(8,128)(2,1)} custom-call(bf16[8,64,1024]{2,1,0:T(8,128)(2,1)S(1)} %all-to-all-done.x_ref, f32[3,1024]{1,0:T(4,128)} %cond_hbm.7, bf16[1024,3072]{1,0:T(8,128)(2,1)} %w_hbm.8), custom_call_target="tpu_custom_call" | custom-call | tf_op jit(solution)/shard_map/temporal/pallas_call | solution.py:293
  30.0 5.4 %all-to-all-start.1 = ((bf16[8,64,512]{2,1,0:T(8,128)(2,1)}), bf16[8,64,512]{2,1,0:T(8,128)(2,1)S(1)}, u32[]{:S(2)}, u32[]{:S(2)}) async-start(bf16[8,64,512]{2,1,0:T(8,128)(2,1)} %temporal.1), calls=%async_computation.1 | async-start | bytes 1048576 | tf_op jit(solution)/shard_map/all_to_all | solution.py:307
  35.5 3.1 %spatial_query.1.q_hbm = bf16[512,512]{1,0:T(8,128)(2,1)} custom-call(bf16[512,1024]{1,0:T(8,128)(2,1)} %get-tuple-element.7.mod_hbm, bf16[1024,3072]{1,0:T(8,128)(2,1)} %w_hbm.8), custom_call_target="tpu_custom_call" | custom-call | tf_op jit(solution)/shard_map/spatial_query/pallas_call | solution.py:286
  38.5 5.2 %all-to-all-done.1 = bf16[8,64,512]{2,1,0:T(8,128)(2,1)S(1)} async-done(((bf16[8,64,512]{2,1,0:T(8,128)(2,1)}), bf16[8,64,512]{2,1,0:T(8,128)(2,1)S(1)}, u32[]{:S(2)}, u32[]{:S(2)}) %all-to-all-start.1) | async-done | bytes 524320 | tf_op jit(solution)/shard_map/all_to_all | solution.py:307
  43.7 0.0 copy-start
  43.7 0.8 %copy-done = bf16[8,64,512]{2,1,0:T(8,128)(2,1)} copy-done((bf16[8,64,512]{2,1,0:T(8,128)(2,1)}, bf16[8,64,512]{2,1,0:T(8,128)(2,1)S(1)}, u32[]{:S(2)}) %copy-start) | copy-done | bytes 524312
  44.5 3.8 %temporal_out.1.acc_hbm = f32[512,1024]{1,0:T(8,128)} custom-call(bf16[512,512]{1,0:T(8,128)(2,1)} %bitcast.4, bf16[1024,1024]{1,0:T(8,128)(2,1)} %w_hbm.9, bf16[1,512,1024]{2,1,0:T(8,128)(2,1)} %x_hbm.3, f32[3,1024]{1,0:T(4,128)} %cond_hbm.7), custom_call_target="tpu_custom_call" | custom-call | tf_op jit(solution)/shard_map/temporal_out/pallas_call | solution.py:308
  48.3 0.0 collective-permute-done.1.right_ref
  48.3 0.0 collective-permute-done.left_ref
  48.4 6.5 %finish.1 = bf16[1,512,1024]{2,1,0:T(8,128)(2,1)} custom-call(s32[4,4]{1,0:T(4,128)} %nb_hbm.1, s32[4]{0:T(128)} %cnt_hbm.1, f32[512,1024]{1,0:T(8,128)} %temporal_out.1.acc_hbm, f32[3,1024]{1,0:T(4,128)} %cond_hbm.7, s32[1,512]{1,0:T(1,128)} %bitcast.6, bf16[512,512]{1,0:T(8,128)(2,1)} %spatial_query.1.q_hbm, bf16[512,1024]{1,0:T(8,128)(2,1)} %get-tuple-element.8.kv_hbm, ...), custom_call_target="tpu_custom_call" | custom-call | tf_op jit(solution)/shard_map/finish/pallas_call | solution.py:315
Async XLA Ops:
  0.0 24.0 %all-to-all-start = ((bf16[8,64,1024]{2,1,0:T(8,128)(2,1)}), bf16[8,64,1024]{2,1,0:T(8,128)(2,1)S(1)}, u32[]{:S(2)}, u32[]{:S(2)}) async-start(bf16[8,64,1024]{2,1,0:T(8,128)(2,1)} %bitcast.3), calls=%async_computation | async-start | bytes 2097152 | tf_op jit(solution)/shard_map/all_to_all | solution.py:267
  10.2 38.1 %collective-permute-start.1 = (bf16[512,1024]{1,0:T(8,128)(2,1)}, bf16[512,1024]{1,0:T(8,128)(2,1)S(1)}, u32[]{:S(2)}, u32[]{:S(2)}) collective-permute-start(bf16[512,1024]{1,0:T(8,128)(2,1)} %get-tuple-element.8.kv_hbm), channel_id=1, source_target_pairs={{64,0},{128,64},{192,128},{256,192},{320,256},{384,320},{448,384},... | collective-permute-start | bytes 3145736 | tf_op jit(solution)/shard_map/ppermute | solution.py:285
  22.1 26.2 %collective-permute-start = (bf16[512,1024]{1,0:T(8,128)(2,1)}, bf16[512,1024]{1,0:T(8,128)(2,1)S(1)}, u32[]{:S(2)}, u32[]{:S(2)}) collective-permute-start(bf16[512,1024]{1,0:T(8,128)(2,1)} %get-tuple-element.8.kv_hbm), channel_id=1, source_target_pairs={{0,64},{64,128},{128,192},{192,256},{256,320},{320,384},{384,448},... | collective-permute-start | bytes 3145736 | tf_op jit(solution)/shard_map/ppermute | solution.py:284
  30.0 13.7 %all-to-all-start.1 = ((bf16[8,64,512]{2,1,0:T(8,128)(2,1)}), bf16[8,64,512]{2,1,0:T(8,128)(2,1)S(1)}, u32[]{:S(2)}, u32[]{:S(2)}) async-start(bf16[8,64,512]{2,1,0:T(8,128)(2,1)} %temporal.1), calls=%async_computation.1 | async-start | bytes 1048576 | tf_op jit(solution)/shard_map/all_to_all | solution.py:307
  43.7 0.8 %copy-start = (bf16[8,64,512]{2,1,0:T(8,128)(2,1)}, bf16[8,64,512]{2,1,0:T(8,128)(2,1)S(1)}, u32[]{:S(2)}) copy-start(bf16[8,64,512]{2,1,0:T(8,128)(2,1)S(1)} %all-to-all-done.1) | copy-start | bytes 1572868

commit v6 on v5

--- a/solution.py
+++ b/solution.py
@@ -145,20 +145,32 @@
         out.wait()
 
 
-def temporal_out(t_hbm, w_hbm, x_hbm, cond_hbm, o_ref, t_s, w_s, x_s, cond_ref, sem):
-    tokens, half = t_s.shape
+def temporal_out(t_hbm, w_hbm, x_hbm, cond_hbm, o_hbm, t_s, w_s, x_s, cond_ref, o_s, sem):
+    tokens, width = x_s.shape
+    half = width // 2
     copies = [
         (t_hbm, t_s),
         (w_hbm.at[pl.ds(half, half)], w_s),
+        (cond_hbm, cond_ref),
         (x_hbm.at[0], x_s),
-        (cond_hbm, cond_ref),
     ]
     copies = [pltpu.make_async_copy(a, b, sem.at[i]) for i, (a, b) in enumerate(copies)]
     for c in copies:
         c.start()
     for c in copies:
         c.wait()
-    o_ref[...] = x_s[...].astype(F32) + cond_ref[2:3, :] * dot(t_s[...], w_s[...])
+    gate = cond_ref[2:3, :]
+    heads = t_s[...].reshape(tokens, half)
+    quarter = width // 4
+    outs = []
+    for i in range(4):
+        cs = slice(i * quarter, (i + 1) * quarter)
+        o_s[:, cs] = x_s[:, cs].astype(F32) + gate[:, cs] * dot(heads, w_s[:, cs])
+        out = pltpu.make_async_copy(o_s.at[:, cs], o_hbm.at[:, cs], sem.at[4 + i])
+        out.start()
+        outs.append(out)
+    for out in outs:
+        out.wait()
 
 
 def finish(nb_hbm, cnt_hbm, acc_hbm, cond_hbm, slot_hbm, q_hbm, kv_hbm, left_ref, right_ref, w_hbm, o_hbm,
@@ -246,6 +258,10 @@
     return pltpu.with_memory_space_constraint(x, pltpu.VMEM)
 
 
+def far(x):
+    return pltpu.with_memory_space_constraint(x, pltpu.HBM)
+
+
 def call(kernel, ins, outs, shapes, scratch):
     return pl.pallas_call(
         kernel,
@@ -304,13 +320,20 @@
             DMA((8,)),
         ],
     )(near(seen), cond, w_qkv)
-    back = lax.all_to_all(t_out, "member", 0, 0, tiled=True).reshape(tokens, half)
+    back = far(lax.all_to_all(t_out, "member", 0, 0, tiled=True))
     acc = call(
         temporal_out,
         [HB, HB, HB, HB],
-        VM,
+        HB,
         arr((tokens, width), F32),
-        [room(tokens, half), room(half, width), room(tokens, width), pltpu.VMEM((3, width), F32), DMA((4,))],
+        [
+            room(CLIP, per, half),
+            room(half, width),
+            room(tokens, width),
+            pltpu.VMEM((3, width), F32),
+            pltpu.VMEM((tokens, width), F32),
+            DMA((8,)),
+        ],
     )(back, w_out, latent, cond)
     return call(
         finish,

time: 55.3 us -> 55.2 us (level)
  no operation moved by 1% of the time
where the time goes in v6:
time: 55.2 us; the launch traced here: 54.7 us
  starting transfers between devices  24.5 us (44%)
  Pallas kernels  24.1 us (44%)
  waiting for transfers between devices  5.22 us (9%)
  local copies, waits for them, and re-layouts  0.79 us (1%)
    ppermute x1, starting transfers between devices, body(): lax.ppermute(kv, 'space', [((i + 1) % count, i) for i in range(count)])  11.9 us
    pallas_call x1, Pallas kernels, body(): call(finish, [HB] * 7 + [VM, VM, HB], HB, arr((1, tokens, width), BF16),...  6.55 us
    pallas_call x1, Pallas kernels, body(): call(temporal, [VM, HB, HB], HB, arr((CLIP, per, half), BF16), [pltpu.VME...  5.97 us
    all_to_all x1, starting transfers between devices, body(): back = far(lax.all_to_all(t_out, 'member', 0, 0, tiled=True))  5.43 us
    all_to_all x1, starting transfers between devices, body(): lax.all_to_all(latent.reshape(CLIP, per, width), 'member', 0, 0, tiled=True)  5.31 us
    all_to_all x1, waiting for transfers between devices, body(): back = far(lax.all_to_all(t_out, 'member', 0, 0, tiled=True))  5.21 us
    pallas_call x1, Pallas kernels, body(): call(spatial_keyval, [HB, HB, HB, HB], (HB, HB), (arr((tokens, width), BF...  4.89 us
    pallas_call x1, Pallas kernels, body(): call(temporal_out, [HB, HB, HB, HB], HB, arr((tokens, width), F32), [room...  3.62 us
  transfers between devices with their start and end apart: 4, of which 1 were waited for; matrix products, arithmetic and copies ran while one was open for 0% of the time, Pallas kernels for 32%

profile of v6, /device:TPU:16, one launch (start us, length us, event | category | flops | bytes accessed | tf_op | source)
XLA Modules:
  0.0 54.7 jit_solution(10332653257757344775)
XLA Ops:
  0.0 5.3 %all-to-all-start = ((bf16[8,64,1024]{2,1,0:T(8,128)(2,1)}), bf16[8,64,1024]{2,1,0:T(8,128)(2,1)S(1)}, u32[]{:S(2)}, u32[]{:S(2)}) async-start(bf16[8,64,1024]{2,1,0:T(8,128)(2,1)} %bitcast.2), calls=%async_computation | async-start | bytes 2097152 | tf_op jit(solution)/shard_map/all_to_all | solution.py:283
  5.3 4.9 %spatial_keyval.1 = (bf16[512,1024]{1,0:T(8,128)(2,1)}, bf16[512,1024]{1,0:T(8,128)(2,1)}) custom-call(bf16[1,512,1024]{2,1,0:T(8,128)(2,1)} %x_hbm.3, f32[3,1024]{1,0:T(4,128)} %cond_hbm.7, s32[1,512]{1,0:T(1,128)} %bitcast.3, bf16[1024,3072]{1,0:T(8,128)(2,1)} %w_hbm.8), custom_call_target="tpu_custom_call" | custom-call | tf_op jit(solution)/shard_map/spatial_keyval/pallas_call | solution.py:284
  10.2 11.9 %collective-permute-start.1 = (bf16[512,1024]{1,0:T(8,128)(2,1)}, bf16[512,1024]{1,0:T(8,128)(2,1)S(1)}, u32[]{:S(2)}, u32[]{:S(2)}) collective-permute-start(bf16[512,1024]{1,0:T(8,128)(2,1)} %get-tuple-element.8.kv_hbm), channel_id=1, source_target_pairs={{64,0},{128,64},{192,128},{256,192},{320,256},{384,320},{448,384},... | collective-permute-start | bytes 3145736 | tf_op jit(solution)/shard_map/ppermute | solution.py:301
  22.1 1.9 %collective-permute-start = (bf16[512,1024]{1,0:T(8,128)(2,1)}, bf16[512,1024]{1,0:T(8,128)(2,1)S(1)}, u32[]{:S(2)}, u32[]{:S(2)}) collective-permute-start(bf16[512,1024]{1,0:T(8,128)(2,1)} %get-tuple-element.8.kv_hbm), channel_id=1, source_target_pairs={{0,64},{64,128},{128,192},{192,256},{256,320},{320,384},{384,448},... | collective-permute-start | bytes 3145736 | tf_op jit(solution)/shard_map/ppermute | solution.py:300
  24.0 0.0 all-to-all-done.x_ref
  24.0 6.0 %temporal.1 = bf16[8,64,512]{2,1,0:T(8,128)(2,1)} custom-call(bf16[8,64,1024]{2,1,0:T(8,128)(2,1)S(1)} %all-to-all-done.x_ref, f32[3,1024]{1,0:T(4,128)} %cond_hbm.7, bf16[1024,3072]{1,0:T(8,128)(2,1)} %w_hbm.8), custom_call_target="tpu_custom_call" | custom-call | tf_op jit(solution)/shard_map/temporal/pallas_call | solution.py:309
  30.0 5.4 %all-to-all-start.1 = ((bf16[8,64,512]{2,1,0:T(8,128)(2,1)}), bf16[8,64,512]{2,1,0:T(8,128)(2,1)S(1)}, u32[]{:S(2)}, u32[]{:S(2)}) async-start(bf16[8,64,512]{2,1,0:T(8,128)(2,1)} %temporal.1), calls=%async_computation.1 | async-start | bytes 1048576 | tf_op jit(solution)/shard_map/all_to_all | solution.py:323
  35.5 3.1 %spatial_query.1.q_hbm = bf16[512,512]{1,0:T(8,128)(2,1)} custom-call(bf16[512,1024]{1,0:T(8,128)(2,1)} %get-tuple-element.7.mod_hbm, bf16[1024,3072]{1,0:T(8,128)(2,1)} %w_hbm.8), custom_call_target="tpu_custom_call" | custom-call | tf_op jit(solution)/shard_map/spatial_query/pallas_call | solution.py:302
  38.5 5.2 %all-to-all-done.1.t_hbm = bf16[8,64,512]{2,1,0:T(8,128)(2,1)S(1)} async-done(((bf16[8,64,512]{2,1,0:T(8,128)(2,1)}), bf16[8,64,512]{2,1,0:T(8,128)(2,1)S(1)}, u32[]{:S(2)}, u32[]{:S(2)}) %all-to-all-start.1) | async-done | bytes 524320 | tf_op jit(solution)/shard_map/all_to_all | solution.py:323
  43.7 0.0 copy-start
  43.7 0.8 %copy-done = bf16[8,64,512]{2,1,0:T(8,128)(2,1)} copy-done((bf16[8,64,512]{2,1,0:T(8,128)(2,1)}, bf16[8,64,512]{2,1,0:T(8,128)(2,1)S(1)}, u32[]{:S(2)}) %copy-start) | copy-done | bytes 524312
  44.5 3.6 %temporal_out.1.acc_hbm = f32[512,1024]{1,0:T(8,128)} custom-call(bf16[8,64,512]{2,1,0:T(8,128)(2,1)} %copy-done, bf16[1024,1024]{1,0:T(8,128)(2,1)} %w_hbm.9, bf16[1,512,1024]{2,1,0:T(8,128)(2,1)} %x_hbm.3, f32[3,1024]{1,0:T(4,128)} %cond_hbm.7), custom_call_target="tpu_custom_call" | custom-call | tf_op jit(solution)/shard_map/temporal_out/pallas_call | solution.py:324
  48.2 0.0 collective-permute-done.1.right_ref
  48.2 0.0 collective-permute-done.left_ref
  48.2 6.5 %finish.1 = bf16[1,512,1024]{2,1,0:T(8,128)(2,1)} custom-call(s32[4,4]{1,0:T(4,128)} %nb_hbm.1, s32[4]{0:T(128)} %cnt_hbm.1, f32[512,1024]{1,0:T(8,128)} %temporal_out.1.acc_hbm, f32[3,1024]{1,0:T(4,128)} %cond_hbm.7, s32[1,512]{1,0:T(1,128)} %bitcast.4, bf16[512,512]{1,0:T(8,128)(2,1)} %spatial_query.1.q_hbm, bf16[512,1024]{1,0:T(8,128)(2,1)} %get-tuple-element.8.kv_hbm, ...), custom_call_target="tpu_custom_call" | custom-call | tf_op jit(solution)/shard_map/finish/pallas_call | solution.py:338
Async XLA Ops:
  0.0 24.0 %all-to-all-start = ((bf16[8,64,1024]{2,1,0:T(8,128)(2,1)}), bf16[8,64,1024]{2,1,0:T(8,128)(2,1)S(1)}, u32[]{:S(2)}, u32[]{:S(2)}) async-start(bf16[8,64,1024]{2,1,0:T(8,128)(2,1)} %bitcast.2), calls=%async_computation | async-start | bytes 2097152 | tf_op jit(solution)/shard_map/all_to_all | solution.py:283
  10.2 38.0 %collective-permute-start.1 = (bf16[512,1024]{1,0:T(8,128)(2,1)}, bf16[512,1024]{1,0:T(8,128)(2,1)S(1)}, u32[]{:S(2)}, u32[]{:S(2)}) collective-permute-start(bf16[512,1024]{1,0:T(8,128)(2,1)} %get-tuple-element.8.kv_hbm), channel_id=1, source_target_pairs={{64,0},{128,64},{192,128},{256,192},{320,256},{384,320},{448,384},... | collective-permute-start | bytes 3145736 | tf_op jit(solution)/shard_map/ppermute | solution.py:301
  22.1 26.1 %collective-permute-start = (bf16[512,1024]{1,0:T(8,128)(2,1)}, bf16[512,1024]{1,0:T(8,128)(2,1)S(1)}, u32[]{:S(2)}, u32[]{:S(2)}) collective-permute-start(bf16[512,1024]{1,0:T(8,128)(2,1)} %get-tuple-element.8.kv_hbm), channel_id=1, source_target_pairs={{0,64},{64,128},{128,192},{192,256},{256,320},{320,384},{384,448},... | collective-permute-start | bytes 3145736 | tf_op jit(solution)/shard_map/ppermute | solution.py:300
  30.0 13.7 %all-to-all-start.1 = ((bf16[8,64,512]{2,1,0:T(8,128)(2,1)}), bf16[8,64,512]{2,1,0:T(8,128)(2,1)S(1)}, u32[]{:S(2)}, u32[]{:S(2)}) async-start(bf16[8,64,512]{2,1,0:T(8,128)(2,1)} %temporal.1), calls=%async_computation.1 | async-start | bytes 1048576 | tf_op jit(solution)/shard_map/all_to_all | solution.py:323
  43.7 0.8 %copy-start = (bf16[8,64,512]{2,1,0:T(8,128)(2,1)}, bf16[8,64,512]{2,1,0:T(8,128)(2,1)S(1)}, u32[]{:S(2)}) copy-start(bf16[8,64,512]{2,1,0:T(8,128)(2,1)S(1)} %all-to-all-done.1.t_hbm) | copy-start | bytes 1572868
